TPU v7x, 128 devices: a whole 4x4x4 slice. The times are simulated.
128 devices in a mesh: grp: 2 (over z_lo), wide: 64 (over z_hi, y, x, core).
Axes of the slice: x: 4, y: 4, z: 4 (z_hi: 2, z_lo: 2; z = z_hi * 2 + z_lo), core: 2. Of those that a mesh axis runs over, the one named last changes fastest.
Arguments:
- tile_values: bfloat16 [1024, 512, 512], P('wide', None, 'grp'), may hold values from -200 to 1000
- tile_rows: int32 [1024], P('wide'), may hold values from 0 to 255, as said below
- tile_cols: int32 [1024], P('wide'), may hold values from 0 to 511, as said below
- objective: float32 [512, 512], P('wide', 'grp'), may hold values from -40 to 42
- demand: float32 [256, 512], P('wide', 'grp'), may hold values from -40 to 42
- primal_step: float32 [], replicated, may hold values from 0.5 to 0.95
- dual_step: float32 [], replicated, may hold values from 0.5 to 0.95
Outputs:
- primal_iterate: float32 [512, 512], P('wide', 'grp')
- dual_iterate: float32 [256, 512], P('wide', 'grp')
Inputs may be any that keep to these rules, and one draw needn't show every extreme that they name: `tile_rows`: every block row is named by at least one tile; tiles may repeat a block position, and then they add. `tile_cols`: the 16 tiles held by index w of wide all lie in block columns w * 8 to (w + 1) * 8 - 1, and each of these columns is named by at least one of them.
All inputs are finite; a program needn't handle non-finite values.
Results may differ from a plain program's by a relative error of at most 0.0003.
Values may be sent and summed in bfloat16 or wider, within the bound.
A program may use at most 64 MiB of HBM per device.

v0:
```python
import jax
import jax.numpy as jnp
from jax import lax
from jax.sharding import Mesh
from jax.sharding import PartitionSpec as P

PASSES = 2
ITERS = 2
WIDE = ("wide_0", "wide_1", "wide_2", "wide_3")
GRP_WIDE = ("grp", "wide_0", "wide_1", "wide_2", "wide_3")


HIGHEST = lax.Precision.HIGHEST
EPSILON = 1e-06


def over_axes(value, axes):
    for axis in axes:
        value = lax.psum(value, axis)
    return value


def cut_along(value, dim, count):
    before, after = (value.shape[:dim], value.shape[dim + 1 :])
    return jnp.moveaxis(value.reshape(*before, count, -1, *after), dim, 0)


def sum_at_owner(value, axis, dim):
    count = lax.axis_size(axis)
    parts = lax.all_to_all(cut_along(value, dim, count), axis, 0, 0, tiled=True)
    return jnp.sum(parts, axis=0)


def laid_out(parts, dim):
    parts = jnp.moveaxis(parts, 0, dim)
    dims = parts.shape
    return parts.reshape(*dims[:dim], dims[dim] * dims[dim + 1], *dims[dim + 2 :])


def from_everyone(value, axis):
    copies = jnp.broadcast_to(value, (lax.axis_size(axis), *value.shape))
    return lax.all_to_all(copies, axis, split_axis=0, concat_axis=0, tiled=True)


def gather_directly(value, axis, dim):
    return laid_out(from_everyone(value, axis), dim)


def select(onehot, values):
    return jnp.dot(onehot, values, precision=HIGHEST, preferred_element_type=jnp.float32)


def on_device(tile_values, tile_rows, tile_cols, objective, demand, primal_step, dual_step):
    blocks, block_size, half_width = tile_values.shape
    col_local = objective.shape[0]
    row_local = demand.shape[0]
    wide_count = lax.axis_size(WIDE)
    row_count = row_local * wide_count
    wide_index = lax.axis_index(WIDE)
    grp_index = lax.axis_index("grp")
    local_cols = tile_cols - wide_index * col_local
    row_table = (tile_rows[None, :] == jnp.arange(row_count, dtype=jnp.int32)[:, None]).astype(
        jnp.float32
    )
    col_table = (local_cols[None, :] == jnp.arange(col_local, dtype=jnp.int32)[:, None]).astype(
        jnp.float32
    )
    magnitude = jnp.abs(tile_values)
    row_factor = jnp.ones((row_count, block_size), jnp.float32)
    col_factor = jnp.ones((col_local, half_width), jnp.float32)
    for repeat_index in range(PASSES):
        row_pick = select(row_table.T, row_factor).astype(jnp.bfloat16)
        col_pick = select(col_table.T, col_factor).astype(jnp.bfloat16)
        row_part = jnp.einsum("kij,kj->ki", magnitude, col_pick, preferred_element_type=jnp.float32)
        col_part = jnp.einsum("kij,ki->kj", magnitude, row_pick, preferred_element_type=jnp.float32)
        col_total = select(col_table, col_part)
        row_sum = select(row_table, row_part)
        row_total = lax.psum(row_sum, GRP_WIDE)
        row_next = row_factor / jnp.sqrt(row_factor * row_total + EPSILON)
        col_factor = col_factor / jnp.sqrt(col_factor * col_total + EPSILON)
        row_factor = row_next
    row_pick = select(row_table.T, row_factor)
    col_pick = select(col_table.T, col_factor)
    scaled = (row_pick[:, :, None] * tile_values.astype(jnp.float32) * col_pick[:, None, :]).astype(
        jnp.bfloat16
    )
    own_rows = lax.dynamic_slice(
        row_factor, (wide_index * row_local, grp_index * half_width), (row_local, half_width)
    )
    cost_scaled = col_factor * objective
    demand_scaled = own_rows * demand
    cost_square, demand_square = (
        over_axes(jnp.sum(cost_scaled * cost_scaled), GRP_WIDE),
        over_axes(jnp.sum(demand_scaled * demand_scaled), GRP_WIDE),
    )
    cost_hat = cost_scaled / jnp.sqrt(cost_square / (col_local * wide_count * block_size) + EPSILON)
    demand_hat = demand_scaled / jnp.sqrt(demand_square / (row_count * block_size) + EPSILON)
    primal = jnp.zeros((col_local, half_width), jnp.float32)
    dual = jnp.zeros((row_local, half_width), jnp.float32)
    col_pickup = col_table.T.astype(jnp.bfloat16)
    row_pickup = row_table.T.astype(jnp.bfloat16)
    relaid = lax.all_to_all(scaled, "grp", split_axis=1, concat_axis=2, tiled=True)

    def row_terms_of(values, amount):
        row_ids = jnp.arange(amount, dtype=jnp.int32)
        row_onehot = (tile_rows[None, :] == row_ids[:, None]).astype(jnp.float32)
        return select(row_onehot, values)

    col_abs = sum_at_owner(
        select(col_table, jnp.sum(jnp.abs(relaid), axis=1, dtype=jnp.float32)), "grp", 1
    )
    row_abs = sum_at_owner(
        row_terms_of(
            jnp.sum(jnp.abs(relaid), axis=2, dtype=jnp.float32), row_local * lax.axis_size(WIDE)
        ),
        WIDE,
        0,
    )
    primal_rate = primal_step / (col_abs + EPSILON)
    dual_rate = dual_step / (row_abs + EPSILON)
    for iteration in range(ITERS):
        dual_half = gather_directly(dual.astype(jnp.bfloat16), WIDE, 0)
        dual_pick = jnp.dot(row_pickup, dual_half, preferred_element_type=jnp.float32).astype(
            jnp.bfloat16
        )
        column_terms = jnp.einsum(
            "kij,ki->kj", relaid, dual_pick, preferred_element_type=jnp.float32
        )
        pulled = sum_at_owner(select(col_table, column_terms), "grp", 1)
        primal_next = jnp.maximum(primal - primal_rate * (cost_hat - pulled), 0.0)
        primal_bar = (2.0 * primal_next - primal).astype(jnp.bfloat16)
        primal_full = gather_directly(primal_bar, "grp", 1)
        primal_pick = jnp.dot(col_pickup, primal_full, preferred_element_type=jnp.float32).astype(
            jnp.bfloat16
        )
        products = jnp.einsum("kij,kj->ki", relaid, primal_pick, preferred_element_type=jnp.float32)
        pushed = sum_at_owner(row_terms_of(products, row_local * lax.axis_size(WIDE)), WIDE, 0)
        dual = dual + dual_rate * (demand_hat - pushed)
        primal = primal_next
    return (primal, dual)


def solution(mesh):
    split = Mesh(
        mesh.devices.reshape(mesh.shape["grp"], 2, 4, 4, 2),
        ("grp", "wide_0", "wide_1", "wide_2", "wide_3"),
    )
    placed = (P(WIDE, None, "grp"), P(WIDE), P(WIDE), P(WIDE, "grp"), P(WIDE, "grp"), P(), P())
    return jax.shard_map(
        on_device,
        mesh=split,
        in_specs=placed,
        out_specs=(P(WIDE, "grp"), P(WIDE, "grp")),
        check_vma=False,
    )
```

profile of v0, /device:TPU:0, one launch (start us, length us, event | category | flops | bytes accessed | tf_op | source)
XLA Modules:
  0.0 401.7 jit_solution(5926019624456735458)
XLA Ops:
  7.2 0.9 fusion.10
  8.1 0.8 broadcast_subtract_fusion
  9.1 3.2 fusion.4
  12.4 1.2 fusion.6
  13.6 1.2 fusion.26
  15.0 1.2 fusion.2
  16.2 1.2 fusion.25
  17.4 150.4 %all-reduce.8.cloned.1.call-done = (f32[256,512]{1,0:T(8,128)}, f32[256,512]{1,0:T(8,128)}) async-done(((f32[256,512]{1,0:T(8,128)}, f32[256,512]{1,0:T(8,128)}), (f32[256,512]{1,0:T(8,128)}, f32[256,512]{1,0:T(8,128)})) %all-reduce.8.cloned.1.call-update) | async-done | bytes 1048592 | tf_op jit(solution)/shard_map/psum | solution.py:78
  167.8 1.5 fusion.11
  169.4 2.9 fusion
  172.3 0.7 multiply_reduce_fusion
  173.2 1.2 rsqrt_multiply_fusion
  174.4 0.6 fusion.24
  175.0 10.3 %multiply_convert_fusion = bf16[16,512,256]{2,0,1:T(8,128)(2,1)} fusion(bf16[16,512,256]{2,1,0:T(8,128)(2,1)S(1)} %copy-done.1, f32[16,256]{1,0:T(8,128)S(1)} %fusion.78, f32[16,512]{0,1:T(8,128)S(1)} %fusion.24), kind=kLoop, calls=%fused_computation.2 | loop fusion | flops 8388608 | bytes 8437760 | tf_op jit(solution)/shard_map/convert_element_type | solution.py:84
  185.3 5.7 %all-to-all-start = ((bf16[16,512,256]{2,0,1:T(8,128)(2,1)}), bf16[16,512,256]{2,0,1:T(8,128)(2,1)}, u32[]{:S(2)}, u32[]{:S(2)}) async-start(bf16[16,512,256]{2,0,1:T(8,128)(2,1)} %multiply_convert_fusion), calls=%async_computation | async-start | bytes 8388608 | tf_op jit(solution)/shard_map/all_to_all | solution.py:102
  191.9 0.7 multiply_reduce_fusion.1
  192.6 47.4 %all-reduce.5 = (f32[]{:T(128)}, f32[]{:T(128)}) all-reduce(f32[]{:T(128)} %get-tuple-element.18, f32[]{:T(128)} %multiply_reduce_fusion.1), channel_id=1, replica_groups=mesh['grp'=2,'wide_0'=2,'wide_1'=4,'wide_2'=4,'wide_3'=2] {'grp'}, use_global_device_ids=true, to_apply=%region_5.0 | all-reduce | flops 2 | bytes 16 | tf_op jit(solution)/shard_map/psum | solution.py:19
  240.0 7.0 %all-reduce.4 = (f32[]{:T(128)}, f32[]{:T(128)}) all-reduce(f32[]{:T(128)} %get-tuple-element.12, f32[]{:T(128)} %get-tuple-element.13), channel_id=1, replica_groups=mesh['grp'=2,'wide_0'=2,'wide_1'=4,'wide_2'=4,'wide_3'=2] {'wide_0'}, use_global_device_ids=true, to_apply=%region_6.0 | all-reduce | flops 2 | bytes 16 | tf_op jit(solution)/shard_map/psum | solution.py:19
  247.0 10.7 %all-reduce.2 = (f32[]{:T(128)}, f32[]{:T(128)}) all-reduce(f32[]{:T(128)} %get-tuple-element.10, f32[]{:T(128)} %get-tuple-element.11), channel_id=1, replica_groups=mesh['grp'=2,'wide_0'=2,'wide_1'=4,'wide_2'=4,'wide_3'=2] {'wide_1'}, use_global_device_ids=true, to_apply=%region_7.0 | all-reduce | flops 2 | bytes 16 | tf_op jit(solution)/shard_map/psum | solution.py:19
  257.8 10.4 %all-reduce.1 = (f32[]{:T(128)}, f32[]{:T(128)}) all-reduce(f32[]{:T(128)} %get-tuple-element.6, f32[]{:T(128)} %get-tuple-element.7), channel_id=1, replica_groups=mesh['grp'=2,'wide_0'=2,'wide_1'=4,'wide_2'=4,'wide_3'=2] {'wide_2'}, use_global_device_ids=true, to_apply=%region_8.0 | all-reduce | flops 2 | bytes 16 | tf_op jit(solution)/shard_map/psum | solution.py:19
  268.2 3.1 all-reduce.3
  272.1 7.5 %copy.16 = bf16[16,256,2,256]{1,3,2,0:T(8,128)(2,1)} copy(bf16[16,256,2,256]{3,0,1,2:T(8,128)(2,1)} %bitcast.14) | data formatting | bytes 8388608 | tf_op jit(solution)/shard_map/all_to_all | solution.py:102
  279.6 3.4 fusion.64
  283.0 0.7 fusion.39
  283.7 3.4 all-to-all-start.2
  287.1 4.4 %convert_reduce_fusion.1 = f32[16,2,256]{2,1,0:T(2,128)S(1)} fusion(bf16[16,512,256]{2,0,1:T(8,128)(2,1)} %all-to-all-done), kind=kLoop, calls=%fused_computation.1 | loop fusion | flops 6283264 | bytes 4227072 | tf_op jit(solution)/shard_map/reduce_sum | solution.py:110
  291.5 0.7 convolution_bitcast_fusion
  292.3 5.6 %copy.14 = bf16[16,512,256]{2,1,0:T(8,128)(2,1)} copy(bf16[16,512,256]{2,0,1:T(8,128)(2,1)} %all-to-all-done) | data formatting | bytes 8388608 | tf_op jit(solution)/shard_map/all_to_all | solution.py:102
  297.9 3.2 all-to-all-start.1
  301.1 3.1 convert_reduce_fusion
  304.2 0.7 all-to-all-done.1
  305.6 3.2 all-to-all-start.4
  309.2 0.9 copy.17
  310.1 2.5 all-to-all-done.4
  312.6 4.6 %all-to-all-start.3 = ((f32[64,4,256]{2,1,0:T(4,128)}), f32[64,4,256]{2,1,0:T(4,128)S(1)}, u32[]{:S(2)}, u32[]{:S(2)}) async-start(f32[64,4,256]{2,1,0:T(4,128)} %copy.17), calls=%async_computation.3 | async-start | bytes 524288 | tf_op jit(solution)/shard_map/all_to_all | solution.py:30
  317.4 2.8 fusion.46
  320.5 0.8 reshape.53
  321.3 7.2 %all-to-all-done.3 = f32[64,4,256]{2,1,0:T(4,128)S(1)} async-done(((f32[64,4,256]{2,1,0:T(4,128)}), f32[64,4,256]{2,1,0:T(4,128)S(1)}, u32[]{:S(2)}, u32[]{:S(2)}) %all-to-all-start.3) | async-done | bytes 262176 | tf_op jit(solution)/shard_map/all_to_all | solution.py:30
  328.5 4.6 %all-to-all-start.5 = ((f32[64,4,256]{2,1,0:T(4,128)}), f32[64,4,256]{2,1,0:T(4,128)S(1)}, u32[]{:S(2)}, u32[]{:S(2)}) async-start(f32[64,4,256]{2,1,0:T(4,128)} %reshape.53), calls=%async_computation.5 | async-start | bytes 524288 | tf_op jit(solution)/shard_map/all_to_all | solution.py:30
  334.5 9.8 %all-to-all-done.5 = f32[64,4,256]{2,1,0:T(4,128)S(1)} async-done(((f32[64,4,256]{2,1,0:T(4,128)}), f32[64,4,256]{2,1,0:T(4,128)S(1)}, u32[]{:S(2)}, u32[]{:S(2)}) %all-to-all-start.5) | async-done | bytes 262176 | tf_op jit(solution)/shard_map/all_to_all | solution.py:30
  344.6 14.0 %all_to_all.64 = bf16[64,4,256]{2,1,0:T(4,128)(2,1)S(1)} all-to-all(bf16[64,4,256]{2,1,0:T(4,128)(2,1)S(1)} %broadcast_in_dim.13), channel_id=1, replica_groups=mesh['grp'=2,'wide_0'=2,'wide_1'=4,'wide_2'=4,'wide_3'=2] {'wide_0','wid..., dimensions={0} | all-to-all | bytes 262144 | tf_op jit(solution)/shard_map/all_to_all | solution.py:42
  358.8 3.4 fusion.61
  362.4 6.2 %all_to_all.65 = f32[2,8,256]{2,1,0:T(8,128)S(1)} all-to-all(f32[2,8,256]{2,1,0:T(8,128)S(1)} %bitcast.95), channel_id=1, replica_groups=mesh['grp'=2,'wide_0'=2,'wide_1'=4,'wide_2'=4,'wide_3'=2] {'grp'}, dimensions={0} | all-to-all | bytes 32768 | tf_op jit(solution)/shard_map/all_to_all | solution.py:30
  368.6 0.6 subtract_convert_fusion
  369.2 6.1 %all_to_all.66 = bf16[2,8,256]{2,1,0:T(8,128)(2,1)S(1)} all-to-all(bf16[2,8,256]{2,1,0:T(8,128)(2,1)S(1)} %broadcast_in_dim.14), channel_id=1, replica_groups=mesh['grp'=2,'wide_0'=2,'wide_1'=4,'wide_2'=4,'wide_3'=2] {'grp'}, dimensions={0} | all-to-all | bytes 16384 | tf_op jit(solution)/shard_map/all_to_all | solution.py:42
  375.5 2.8 fusion.43
  378.7 15.4 %all_to_all.67 = f32[64,4,256]{2,1,0:T(4,128)S(1)} all-to-all(f32[64,4,256]{2,1,0:T(4,128)S(1)} %reshape.57), channel_id=1, replica_groups=mesh['grp'=2,'wide_0'=2,'wide_1'=4,'wide_2'=4,'wide_3'=2] {'wide_0','wid..., dimensions={0} | all-to-all | bytes 524288 | tf_op jit(solution)/shard_map/all_to_all | solution.py:30
  394.1 0.7 multiply_add_fusion
  (42 shorter events, 3.7 us)
Async XLA Ops:
  7.2 160.6 %all-reduce.8.cloned.1.call-start = ((), (), s32[]{:S(2)}) async-start(), calls=%async_computation.10 | async-start | bytes 2097152 | tf_op jit(solution)/shard_map/psum | solution.py:78
  8.1 4.3 %copy-start = (bf16[16,512,256]{2,1,0:T(8,128)(2,1)S(1)}, bf16[16,512,256]{2,1,0:T(8,128)(2,1)}, u32[]{:S(2)}) copy-start(bf16[16,512,256]{2,1,0:T(8,128)(2,1)} %param.7) | copy-start | bytes 12582916
  9.1 4.5 %copy-start.4 = (s32[16]{0:T(128)S(1)}, s32[16]{0:T(128)}, u32[]{:S(2)}) copy-start(s32[16]{0:T(128)} %param.8) | copy-start | bytes 196
  16.2 156.1 %copy-start.5 = (f32[8,256]{1,0:T(8,128)S(1)}, f32[8,256]{1,0:T(8,128)}, u32[]{:S(2)}) copy-start(f32[8,256]{1,0:T(8,128)} %param.10) | copy-start | bytes 24580
  167.8 5.4 %copy-start.2 = (f32[256,512]{1,0:T(8,128)S(1)}, f32[256,512]{1,0:T(8,128)}, u32[]{:S(2)}) copy-start(f32[256,512]{1,0:T(8,128)} %get-tuple-element.2) | copy-start | bytes 1572868
  167.8 7.2 %copy-start.1 = (bf16[16,512,256]{2,1,0:T(8,128)(2,1)S(1)}, bf16[16,512,256]{2,1,0:T(8,128)(2,1)}, u32[]{:S(2)}) copy-start(bf16[16,512,256]{2,1,0:T(8,128)(2,1)} %param.7) | copy-start | bytes 12582916
  185.3 6.6 %copy-start.3 = (f32[4,256]{1,0:T(4,128)S(1)}, f32[4,256]{1,0:T(4,128)}, u32[]{:S(2)}) copy-start(f32[4,256]{1,0:T(4,128)} %param.11) | copy-start | bytes 12292
  185.3 86.7 %all-to-all-start = ((bf16[16,512,256]{2,0,1:T(8,128)(2,1)}), bf16[16,512,256]{2,0,1:T(8,128)(2,1)}, u32[]{:S(2)}, u32[]{:S(2)}) async-start(bf16[16,512,256]{2,0,1:T(8,128)(2,1)} %multiply_convert_fusion), calls=%async_computation | async-start | bytes 8388608 | tf_op jit(solution)/shard_map/all_to_all | solution.py:102
  283.7 14.2 %all-to-all-start.2 = ((f32[2,8,256]{2,1,0:T(8,128)}), f32[2,8,256]{2,1,0:T(8,128)S(1)}, u32[]{:S(2)}, u32[]{:S(2)}) async-start(f32[2,8,256]{2,1,0:T(8,128)} %bitcast.19), calls=%async_computation.2 | async-start | bytes 32768 | tf_op jit(solution)/shard_map/all_to_all | solution.py:30
  297.9 7.1 %all-to-all-start.1 = ((f32[2,8,256]{2,1,0:T(8,128)}), f32[2,8,256]{2,1,0:T(8,128)S(1)}, u32[]{:S(2)}, u32[]{:S(2)}) async-start(f32[2,8,256]{2,1,0:T(8,128)} %convolution_bitcast_fusion), calls=%async_computation.1 | async-start | bytes 32768 | tf_op jit(solution)/shard_map/all_to_all | solution.py:30
  305.6 7.0 %all-to-all-start.4 = ((bf16[2,8,256]{2,1,0:T(8,128)(2,1)}), bf16[2,8,256]{2,1,0:T(8,128)(2,1)S(1)}, u32[]{:S(2)}, u32[]{:S(2)}) async-start(bf16[2,8,256]{2,1,0:T(8,128)(2,1)} %broadcast_in_dim.12), calls=%async_computation.4 | async-start | bytes 16384 | tf_op jit(solution)/shard_map/all_to_all | solution.py:42
  312.6 15.9 %all-to-all-start.3 = ((f32[64,4,256]{2,1,0:T(4,128)}), f32[64,4,256]{2,1,0:T(4,128)S(1)}, u32[]{:S(2)}, u32[]{:S(2)}) async-start(f32[64,4,256]{2,1,0:T(4,128)} %copy.17), calls=%async_computation.3 | async-start | bytes 524288 | tf_op jit(solution)/shard_map/all_to_all | solution.py:30
  328.5 15.9 %all-to-all-start.5 = ((f32[64,4,256]{2,1,0:T(4,128)}), f32[64,4,256]{2,1,0:T(4,128)S(1)}, u32[]{:S(2)}, u32[]{:S(2)}) async-start(f32[64,4,256]{2,1,0:T(4,128)} %reshape.53), calls=%async_computation.5 | async-start | bytes 524288 | tf_op jit(solution)/shard_map/all_to_all | solution.py:30
Sparse Core Ops, SparseCore 0:
  17.5 150.2 all-reduce.7
where the time goes:
time: 404 us; the launch traced here: 402 us
  waiting for transfers between devices  171 us (42%)
  blocking collectives  120 us (30%)
  matrix products  31 us (8%)
  starting transfers between devices  24.9 us (6%)
  other arithmetic  22.1 us (5%)
  between operations  16.9 us (4%)
  local copies, waits for them, and re-layouts  15.6 us (4%)
    psum x1, waiting for transfers between devices, on_device(): row_total = lax.psum(row_sum, GRP_WIDE)  150 us
    psum x5, blocking collectives, over_axes(): value = lax.psum(value, axis)  78.7 us
    all_to_all x2, blocking collectives, sum_at_owner(): parts = lax.all_to_all(cut_along(value, dim, count), axis, 0, 0, tiled=True)  21.6 us
    all_to_all x2, blocking collectives, from_everyone(): return lax.all_to_all(copies, axis, split_axis=0, concat_axis=0, tiled=True)  20.2 us
    all_to_all x4, waiting for transfers between devices, sum_at_owner(): parts = lax.all_to_all(cut_along(value, dim, count), axis, 0, 0, tiled=True)  17.8 us
    all_to_all x4, starting transfers between devices, sum_at_owner(): parts = lax.all_to_all(cut_along(value, dim, count), axis, 0, 0, tiled=True)  15.9 us
    all_to_all x2, local copies, waits for them, and re-layouts, on_device(): lax.all_to_all(scaled, 'grp', split_axis=1, concat_axis=2, tiled=True)  13.2 us
    convert_element_type x1, other arithmetic, on_device(): (row_pick[:, :, None] * tile_values.astype(jnp.float32) * col_pick[:, Non...  10.3 us
  transfers between devices with their start and end apart: 7, of which 5 were waited for; matrix products, arithmetic and copies ran while one was open for 5% of the time, Pallas kernels for 0%

commit v1 on v0

v1 whole, which is shorter than its diff:
```python
import functools

import jax
import jax.numpy as jnp
from jax import lax
from jax.experimental import pallas as pl
from jax.experimental.pallas import tpu as pltpu
from jax.sharding import Mesh
from jax.sharding import PartitionSpec as P

AXES = ("grp", "zh", "y", "x", "core")
WIDE = AXES[1:]
EPSILON = 1e-06
MESH = pl.DeviceIdType.MESH
F32 = jnp.float32
BF16 = jnp.bfloat16
TILES = 16
CHUNK = 4

(E0, A1Q0, A1Q1, B1, B2, A2, SA, SB, A3Q0, A3Q1, B3, B4, A4, A5, B5) = range(15)
STAGES = 15


def iota(shape, dim):
    return lax.broadcasted_iota(jnp.int32, shape, dim)


def one_hot(condition):
    return jnp.where(condition, 1.0, 0.0).astype(BF16)


def split(value):
    high = value.astype(BF16)
    return high, (value - high.astype(F32)).astype(BF16)


def wait_bytes(ref, sem):
    pltpu.make_async_copy(ref, ref, sem).wait()


def dot(left, right):
    return lax.dot_general(left, right, (((1,), (0,)), ((), ())), preferred_element_type=F32)


def dot_nt(left, right):
    return lax.dot_general(left, right, (((1,), (1,)), ((), ())), preferred_element_type=F32)


def kernel(
    tile_rows,
    tile_cols,
    primal_step,
    dual_step,
    tiles_hbm,
    objective,
    demand,
    primal_out,
    dual_out,
    tiles,
    names,
    names_in,
    row_parts,
    buf_a1,
    buf_a3,
    buf_a5,
    send_b1,
    recv_b1,
    send_b3,
    recv_b3,
    send_b5,
    recv_b5,
    pay2,
    rows2,
    sel2,
    recv_a2,
    pay4,
    rows4,
    sel4,
    recv_a4,
    picked,
    hot1,
    hot2,
    hot4,
    hot5,
    scal,
    scal_a,
    scal_b_out,
    scal_b,
    demand8,
    pushed4,
    tile_sem,
    send_sem,
    recv_sem,
):
    g, zh, y, x, c = (lax.axis_index(axis) for axis in AXES)
    slot_me = (zh * 4 + y) * 2 + c

    def x_device(step):
        return (g, zh, y, lax.rem(x + step, 4), c)

    def plane(step):
        og, oc, oz, oy = (step & 1, (step >> 1) & 1, (step >> 2) & 1, step >> 3)
        return (
            lax.rem(g + og, 2),
            lax.rem(zh + oz, 2),
            lax.rem(y + oy, 4),
            lax.rem(c + oc, 2),
        )

    def send(src, dst, stage, device):
        pltpu.make_async_remote_copy(
            src_ref=src,
            dst_ref=dst,
            send_sem=send_sem.at[stage],
            recv_sem=recv_sem.at[stage],
            device_id=device,
            device_id_type=MESH,
        ).start()

    barrier = pltpu.get_barrier_semaphore()
    for step in range(1, 4):
        pl.semaphore_signal(barrier, inc=1, device_id=x_device(step), device_id_type=MESH)
    for step in range(1, 32):
        pg, pz, py, pc = plane(step)
        pl.semaphore_signal(barrier, inc=1, device_id=(pg, pz, py, x, pc), device_id_type=MESH)

    for chunk in range(TILES // CHUNK):
        part = pl.ds(chunk * CHUNK, CHUNK)
        pltpu.make_async_copy(tiles_hbm.at[part], tiles.at[part], tile_sem.at[chunk]).start()

    sub = iota((16, 128), 0)
    lane = iota((8, 128), 1)
    down = jnp.zeros((16, 128), jnp.int32)
    along = jnp.zeros((8, 128), jnp.int32)
    for k in range(TILES):
        down = jnp.where(sub == k, tile_rows[k], down)
        along = jnp.where((lane & 15) == k, tile_rows[k], along)
    names[0:16, :] = down
    names[16:24, :] = along
    demand8[0:4, :] = demand[...]
    demand8[4:8, :] = demand[...]

    ones_row = jnp.ones((16, 256), BF16)
    ones_col = jnp.ones((16, CHUNK * 512), BF16)
    eight = iota((8, 256), 0)

    def chunk_of(first):
        return tiles[pl.ds(first, CHUNK)].reshape(CHUNK * 512, 256)

    col_total = jnp.zeros((8, 256), F32)
    for chunk in range(TILES // CHUNK):
        part = pl.ds(chunk * CHUNK, CHUNK)
        pltpu.make_async_copy(tiles_hbm.at[part], tiles.at[part], tile_sem.at[chunk]).wait()
        block = jnp.abs(chunk_of(chunk * CHUNK))
        sums = dot_nt(ones_row, block)
        for j in range(CHUNK):
            k = chunk * CHUNK + j
            row_parts[k : k + 1, :] = sums[0:1, j * 512 : (j + 1) * 512]
            column = dot(ones_col[:, :512], block[j * 512 : (j + 1) * 512])
            col_total += jnp.where(eight == tile_cols[k], column[0:8], 0.0)

    pl.semaphore_wait(barrier, 34)

    def to_x(buf, rows, stage):
        for step in range(1, 4):
            send(buf.at[0, rows], buf.at[step, rows], stage, x_device(step))

    def to_plane(src, width, dst, stage):
        for step in range(31, 0, -1):
            pg, pz, py, pc = plane(step)
            target = (pz * 4 + py) * 2 + pc
            lanes = pl.ds(pl.multiple_of(pg * width, width), width)
            send(src.at[target, :, lanes], dst.at[step - 1], stage, (pg, pz, py, x, pc))

    def share(buf, base, stage):
        high, low = split(row_parts[...])
        buf[0, base : base + 16, :] = high
        buf[0, base + 16 : base + 32, :] = low
        to_x(buf, pl.ds(base, 32), stage)

    for step in range(1, 4):
        send(names, names_in.at[step - 1], E0, x_device(step))
    share(buf_a1, 0, A1Q0)

    row16 = iota((16, 512), 0) & 7

    def row_products(left, magnitude):
        def body(step, carry):
            first = step * CHUNK
            block = chunk_of(first)
            if magnitude:
                block = jnp.abs(block)
            sums = dot_nt(left, block)
            for j in range(CHUNK):
                mine = jnp.where(
                    row16 == tile_cols[first + j], sums[:, j * 512 : (j + 1) * 512], 0.0
                )
                row_parts[pl.ds(first + j, 1), :] = jnp.sum(mine, axis=0, keepdims=True)
            return carry

        lax.fori_loop(0, TILES // CHUNK, body, 0)

    eight_wide = iota((8, 512), 0)

    def column_products(kinds, magnitude):
        height = 16 * ((kinds + 1) // 2)

        def body(step, total):
            first = step * CHUNK
            lefts = []
            for j in range(CHUNK):
                k = first + j
                mine = eight_wide == tile_cols[k]
                pieces = [
                    jnp.where(mine, picked[pl.ds(kind * 16 + k, 1), :], 0.0)
                    for kind in range(kinds)
                ]
                while len(pieces) * 8 < height:
                    pieces.append(jnp.zeros((8, 512), F32))
                lefts.append(jnp.concatenate(pieces, axis=0).astype(BF16))
            block = chunk_of(first)
            if magnitude:
                block = jnp.abs(block)
            return total + dot(jnp.concatenate(lefts, axis=1), block)

        return lax.fori_loop(0, TILES // CHUNK, body, jnp.zeros((height, 256), F32))

    col_factor = 1.0 / jnp.sqrt(col_total + EPSILON)
    rounded = jnp.concatenate([col_factor, jnp.zeros_like(col_factor)], axis=0).astype(BF16)
    row_products(rounded, True)
    share(buf_a1, 32, A1Q1)

    wait_bytes(names_in, recv_sem.at[E0])
    lane_names = [names[16:17, :]] + [names_in[p, 16:17, :] for p in range(3)]
    down_names = [names[0:16, :]] + [names_in[p, 0:16, :] for p in range(3)]
    low_half = iota((1, 128), 1) < 64
    wide_names = jnp.concatenate(
        [
            jnp.where(low_half, lane_names[0], lane_names[1]),
            jnp.where(low_half, lane_names[2], lane_names[3]),
        ],
        axis=1,
    )
    m = iota((128, 256), 0)
    n = iota((128, 256), 1)

    def row_id(slot, index):
        return ((((slot >> 1) * 4 + x) * 2 + (slot & 1)) * 4) + index

    ids = row_id(m >> 3, m & 3)
    kind = (m >> 2) & 1
    hot1[...] = one_hot(jnp.logical_and(wide_names == ids, ((n >> 5) & 1) == kind))
    quarter = iota((1, 128), 1) >> 5
    narrow = lane_names[3]
    for p in range(3):
        narrow = jnp.where(quarter == p, lane_names[p], narrow)
    narrow = jnp.concatenate([narrow, narrow], axis=1)
    hot5[...] = one_hot(jnp.logical_and(narrow == ids, (n >> 7) == kind))
    n16 = iota((16, 256), 1)
    ids16 = row_id(n16 >> 4, n16 & 3)
    group = (n16 >> 2) & 3
    for p in range(4):
        named = jnp.concatenate([down_names[p], down_names[p]], axis=1) == ids16
        for q, place in enumerate((0, 1, 3)):
            at = p * 48 + q * 16
            hot2[at : at + 16, :] = one_hot(jnp.logical_and(named, group == place))
        for q in range(2):
            at = p * 32 + q * 16
            hot4[at : at + 16, :] = one_hot(jnp.logical_and(named, group == q))

    def to_owner(buf, send_b, recv_b, stage):
        dense = dot(hot1[...], buf[...].reshape(256, 512))
        send_b[...] = dense.reshape(16, 8, 512)
        to_plane(send_b, 256, recv_b, stage)

    def own_total(send_b, recv_b, width, stage):
        mine = send_b[slot_me]
        mine = jnp.where(g == 0, mine[:, :width], mine[:, width:])
        wait_bytes(recv_b, recv_sem.at[stage])
        return mine + jnp.sum(recv_b[...], axis=0)

    def both(total):
        swapped = pltpu.roll(total, 4, 0)
        upper = eight < 4
        return jnp.where(upper, total, swapped), jnp.where(upper, swapped, total)

    wait_bytes(buf_a1.at[1:4, 0:32], recv_sem.at[A1Q0])
    wait_bytes(buf_a1.at[1:4, 32:64], recv_sem.at[A1Q1])
    to_owner(buf_a1, send_b1, recv_b1, B1)
    first_sum, second_sum = both(own_total(send_b1, recv_b1, 256, B1))
    row_first = 1.0 / jnp.sqrt(first_sum + EPSILON)
    row_factor = row_first / jnp.sqrt(row_first * second_sum + EPSILON)
    upper = eight < 4
    zeros8 = jnp.zeros((8, 256), F32)

    def to_holders(pay, rows, stage_b, hot, sel, recv, stage_a):
        kinds = sel.shape[1]
        lanes = pl.ds(pl.multiple_of(g * 256, 256), 256)
        for step in range(31, 0, -1):
            pg, pz, py, pc = plane(step)
            send(pay, rows.at[slot_me, :, lanes], stage_b, (pg, pz, py, x, pc))
        pltpu.make_async_copy(pay, rows.at[slot_me, :, lanes], recv_sem.at[stage_b]).start()
        wait_bytes(rows, recv_sem.at[stage_b])
        chosen = dot(hot[...], rows[...].reshape(256, 512)).astype(BF16)
        sel[...] = chosen.reshape(4, kinds, 512)
        for step in range(1, 4):
            send(sel.at[step], recv.at[step - 1], stage_a, x_device(4 - step))
        own = sel[0].astype(F32)
        wait_bytes(recv, recv_sem.at[stage_a])
        for p in range(3):
            own = own + recv[p].astype(F32)
        picked[0:kinds, :] = own

    high = row_factor.astype(BF16).astype(F32)
    pay2[...] = jnp.concatenate(
        [
            jnp.where(upper, row_first, row_factor),
            jnp.where(upper, 0.0, row_factor - high),
        ],
        axis=0,
    ).astype(BF16)
    to_holders(pay2, rows2, B2, hot2, sel2, recv_a2, A2)

    sums = column_products(3, True)
    col_next = col_factor / jnp.sqrt(col_factor * sums[0:8] + EPSILON)
    col_abs = col_next * (sums[8:16] + sums[16:24])
    primal_rate = primal_step[0] / (col_abs + EPSILON)
    cost_scaled = col_next * objective[...]
    demand_scaled = row_factor * demand8[...]

    def squares(value):
        return jnp.sum(jnp.sum(value * value, axis=0, keepdims=True), axis=1, keepdims=True)

    lanes1 = iota((1, 128), 1)
    scal[...] = jnp.where(
        lanes1 < 64, squares(cost_scaled), squares(jnp.where(upper, demand_scaled, 0.0))
    )
    for step in range(1, 4):
        send(scal, scal_a.at[step - 1], SA, x_device(step))

    def high_low(value):
        top = value.astype(BF16).astype(F32)
        return jnp.concatenate([top, value - top], axis=0).astype(BF16)

    row_products(high_low(col_next), True)
    share(buf_a3, 0, A3Q0)
    unit = jnp.maximum(-primal_rate * cost_scaled, 0.0)
    row_products(high_low(col_next * (2.0 * unit)), False)
    share(buf_a3, 32, A3Q1)

    wait_bytes(scal_a, recv_sem.at[SA])
    scal_b_out[...] = scal[...] + scal_a[0] + scal_a[1] + scal_a[2]
    for step in range(31, 0, -1):
        pg, pz, py, pc = plane(step)
        send(scal_b_out, scal_b.at[step - 1], SB, (pg, pz, py, x, pc))

    wait_bytes(buf_a3.at[1:4, 0:32], recv_sem.at[A3Q0])
    wait_bytes(buf_a3.at[1:4, 32:64], recv_sem.at[A3Q1])
    to_owner(buf_a3, send_b3, recv_b3, B3)
    wait_bytes(scal_b, recv_sem.at[SB])
    both_squares = scal_b_out[...] + jnp.sum(scal_b[...], axis=0)
    wide_count = 64
    cost_gain = 1.0 / jnp.sqrt(both_squares[:, 0:1] / (8 * wide_count * 512) + EPSILON)
    demand_gain = 1.0 / jnp.sqrt(both_squares[:, 64:65] / (4 * wide_count * 512) + EPSILON)
    primal = cost_gain * unit
    cost_hat = cost_scaled * cost_gain
    demand_hat = demand_scaled * demand_gain

    row_abs, pushed = both(own_total(send_b3, recv_b3, 256, B3))
    dual_rate = dual_step[0] / (row_factor * row_abs + EPSILON)
    dual = dual_rate * (demand_hat - row_factor * (pushed * cost_gain))
    weighted = row_factor * dual.astype(BF16).astype(F32)
    top = weighted.astype(BF16).astype(F32)
    pay4[...] = jnp.concatenate(
        [jnp.where(upper, weighted, weighted - top), zeros8], axis=0
    ).astype(BF16)
    to_holders(pay4, rows4, B4, hot4, sel4, recv_a4, A4)

    sums = column_products(2, False)
    pulled = col_next * (sums[0:8] + sums[8:16])
    primal_next = jnp.maximum(primal - primal_rate * (cost_hat - pulled), 0.0)
    primal_out[...] = primal_next
    bar = (2.0 * primal_next - primal).astype(BF16).astype(F32)
    row_products(high_low(col_next * bar), False)
    share(buf_a5, 0, A5)
    wait_bytes(buf_a5.at[1:4], recv_sem.at[A5])
    terms = buf_a5[...].reshape(128, 512)
    terms = jnp.concatenate(
        [
            jnp.concatenate([terms[:, 0:128], terms[:, 256:384]], axis=1),
            jnp.concatenate([terms[:, 128:256], terms[:, 384:512]], axis=1),
        ],
        axis=0,
    )
    send_b5[...] = dot(hot5[...], terms).reshape(16, 8, 256)
    to_plane(send_b5, 128, recv_b5, B5)
    total = own_total(send_b5, recv_b5, 128, B5)
    pushed4[:, 0:128] = total[0:4]
    pushed4[:, 128:256] = total[4:8]
    dual_out[...] = dual[0:4] + dual_rate[0:4] * (
        demand_hat[0:4] - row_factor[0:4] * pushed4[...]
    )

    wait_bytes(names_in, send_sem.at[E0])
    wait_bytes(buf_a1.at[1:4, 0:32], send_sem.at[A1Q0])
    wait_bytes(buf_a1.at[1:4, 32:64], send_sem.at[A1Q1])
    wait_bytes(recv_b1, send_sem.at[B1])
    for rows, pay, stage in ((recv_b1, pay2, B2), (recv_b3, pay4, B4)):
        wait_bytes(rows, send_sem.at[stage])
    wait_bytes(recv_a2, send_sem.at[A2])
    wait_bytes(scal_a, send_sem.at[SA])
    wait_bytes(scal_b, send_sem.at[SB])
    wait_bytes(buf_a3.at[1:4, 0:32], send_sem.at[A3Q0])
    wait_bytes(buf_a3.at[1:4, 32:64], send_sem.at[A3Q1])
    wait_bytes(recv_b3, send_sem.at[B3])
    wait_bytes(recv_a4, send_sem.at[A4])
    wait_bytes(buf_a5.at[1:4], send_sem.at[A5])
    wait_bytes(recv_b5, send_sem.at[B5])


def on_device(tile_values, tile_rows, tile_cols, objective, demand, primal_step, dual_step):
    wide_index = lax.axis_index(WIDE)
    vmem = pl.BlockSpec(memory_space=pltpu.VMEM)
    smem = pl.BlockSpec(memory_space=pltpu.SMEM)
    return pl.pallas_call(
        kernel,
        out_shape=(
            jax.ShapeDtypeStruct(objective.shape, F32),
            jax.ShapeDtypeStruct(demand.shape, F32),
        ),
        in_specs=[smem, smem, smem, smem, pl.BlockSpec(memory_space=pl.ANY), vmem, vmem],
        out_specs=(vmem, vmem),
        scratch_shapes=[
            pltpu.VMEM((TILES, 512, 256), BF16),
            pltpu.VMEM((24, 128), jnp.int32),
            pltpu.VMEM((3, 24, 128), jnp.int32),
            pltpu.VMEM((16, 512), F32),
            pltpu.VMEM((4, 64, 512), BF16),
            pltpu.VMEM((4, 64, 512), BF16),
            pltpu.VMEM((4, 32, 512), BF16),
            pltpu.VMEM((16, 8, 512), F32),
            pltpu.VMEM((31, 8, 256), F32),
            pltpu.VMEM((16, 8, 512), F32),
            pltpu.VMEM((31, 8, 256), F32),
            pltpu.VMEM((16, 8, 256), F32),
            pltpu.VMEM((31, 8, 128), F32),
            pltpu.VMEM((16, 256), BF16),
            pltpu.VMEM((16, 16, 512), BF16),
            pltpu.VMEM((4, 48, 512), BF16),
            pltpu.VMEM((3, 48, 512), BF16),
            pltpu.VMEM((16, 256), BF16),
            pltpu.VMEM((16, 16, 512), BF16),
            pltpu.VMEM((4, 32, 512), BF16),
            pltpu.VMEM((3, 32, 512), BF16),
            pltpu.VMEM((48, 512), F32),
            pltpu.VMEM((128, 256), BF16),
            pltpu.VMEM((192, 256), BF16),
            pltpu.VMEM((128, 256), BF16),
            pltpu.VMEM((128, 256), BF16),
            pltpu.VMEM((1, 128), F32),
            pltpu.VMEM((3, 1, 128), F32),
            pltpu.VMEM((1, 128), F32),
            pltpu.VMEM((31, 1, 128), F32),
            pltpu.VMEM((8, 256), F32),
            pltpu.VMEM((4, 256), F32),
            pltpu.SemaphoreType.DMA((TILES // CHUNK,)),
            pltpu.SemaphoreType.DMA((STAGES,)),
            pltpu.SemaphoreType.DMA((STAGES,)),
        ],
        compiler_params=pltpu.CompilerParams(collective_id=0, has_side_effects=True),
    )(
        tile_rows,
        tile_cols - wide_index * objective.shape[0],
        primal_step.reshape(1),
        dual_step.reshape(1),
        tile_values,
        objective,
        demand,
    )


def solution(mesh):
    devices = mesh.devices.reshape(mesh.shape["grp"], 2, 4, 4, 2)
    return jax.shard_map(
        on_device,
        mesh=Mesh(devices, AXES),
        in_specs=(P(WIDE, None, "grp"), P(WIDE), P(WIDE), P(WIDE, "grp"), P(WIDE, "grp"), P(), P()),
        out_specs=(P(WIDE, "grp"), P(WIDE, "grp")),
        check_vma=False,
    )
```

time: 404 us -> 75 us (0.19)
  waiting for transfers between devices: 171 us -> 0 us
  blocking collectives: 120 us -> 0 us
  Pallas kernels: 0 us -> 68.4 us
  matrix products: 31 us -> 0 us
  starting transfers between devices: 24.9 us -> 0 us
  other arithmetic: 22.1 us -> 1.17 us
  between operations: 16.9 us -> 1.94 us
  local copies, waits for them, and re-layouts: 15.6 us -> 2.56 us
    psum x1 -> x0, waiting for transfers between devices: 150 us -> none  [on_device(): row_total = lax.psum(row_sum, GRP_WIDE)]
    psum x5 -> x0, blocking collectives: 78.7 us -> none  [over_axes(): value = lax.psum(value, axis)]
    pallas_call x0 -> x1, Pallas kernels: none -> 68.4 us  [on_device(): pl.pallas_call(kernel, out_shape=(jax.ShapeDtypeStruct(objective.shape, F...]
    all_to_all x4 -> x0, blocking collectives: 41.7 us -> none  [the longest x2 21.6 us: sum_at_owner(): parts = lax.all_to_all(cut_along(value, dim, count), axis, 0, 0, tiled=True)]
    dot_general x28 -> x0, matrix products: 31 us -> none  [the longest x16 9.37 us: select(): jnp.dot(onehot, values, precision=HIGHEST, preferred_element_type=jnp.flo...]
    all_to_all x6 -> x0, starting transfers between devices: 24.8 us -> none  [the longest x4 15.9 us: sum_at_owner(): parts = lax.all_to_all(cut_along(value, dim, count), axis, 0, 0, tiled=True)]
    all_to_all x6 -> x0, waiting for transfers between devices: 20.3 us -> none  [the longest x4 17.8 us: sum_at_owner(): parts = lax.all_to_all(cut_along(value, dim, count), axis, 0, 0, tiled=True)]
    all_to_all x2 -> x0, local copies, waits for them, and re-layouts: 13.2 us -> none  [on_device(): lax.all_to_all(scaled, 'grp', split_axis=1, concat_axis=2, tiled=True)]
  transfers between devices with their start and end apart: 7 -> 0, of which waited for: 5 -> 0; matrix products, arithmetic and copies ran while one was open for 5% -> 0% of each run, Pallas kernels for 0% -> 0%
where the time goes in v1:
time: 75 us; the launch traced here: 74 us
  Pallas kernels  68.4 us (91%)
  local copies, waits for them, and re-layouts  2.56 us (3%)
  between operations  1.94 us (3%)
  other arithmetic  1.17 us (2%)
    pallas_call x1, Pallas kernels, on_device(): pl.pallas_call(kernel, out_shape=(jax.ShapeDtypeStruct(objective.shape, F...  68.4 us
    unnamed x2, local copies, waits for them, and re-layouts  2.56 us

profile of v1, /device:TPU:0, one launch (start us, length us, event | category | flops | bytes accessed | tf_op | source)
XLA Modules:
  0.0 74.0 jit_solution(5870277269058200295)
XLA Ops:
  1.9 1.2 %broadcast_subtract_fusion.tile_cols = s32[16]{0:T(128)} fusion(s32[16]{0:T(128)} %param.9, s32[]{:T(128)S(6)} %mul.15), kind=kLoop, calls=%fused_computation | loop fusion | flops 16 | bytes 132 | tf_op jit(solution)/shard_map/sub | solution.py:473
  3.1 68.4 %shard_map.86 = (f32[8,256]{1,0:T(8,128)}, f32[4,256]{1,0:T(4,128)}) custom-call(s32[16]{0:T(128)} %tile_rows.1, s32[16]{0:T(128)} %broadcast_subtract_fusion.tile_cols, f32[1]{0:T(128)} %bitcast.2.primal_step, f32[1]{0:T(128)} %bitcast.3.dual_step, bf16[16,512,256]{2,1,0:T(8,128)(2,1)} %tiles_hbm.1, f32[8,256]{1,0:T(8,128)} %objective.1, f32[4,256]{1,0:T(4,128)} %demand.1), custom_call_target="tpu_custom_call" | custom-call | tf_op jit(solution)/shard_map/pallas_call | solution.py:425
  71.5 1.3 %copy.13 = f32[8,256]{1,0:T(8,128)} copy(f32[8,256]{1,0:T(8,128)} %get-tuple-element.4) | data formatting | bytes 16384
  72.8 1.3 %copy.14 = f32[4,256]{1,0:T(4,128)} copy(f32[4,256]{1,0:T(4,128)} %get-tuple-element.5) | data formatting | bytes 8192

commit v2 on v1

v2 whole, which is shorter than its diff:
```python
import functools

import jax
import jax.numpy as jnp
from jax import lax
from jax.experimental import pallas as pl
from jax.experimental.pallas import tpu as pltpu
from jax.sharding import Mesh
from jax.sharding import PartitionSpec as P

AXES = ("grp", "zh", "y", "x", "core")
WIDE = AXES[1:]
EPSILON = 1e-06
MESH = pl.DeviceIdType.MESH
F32 = jnp.float32
BF16 = jnp.bfloat16
TILES = 16
CHUNK = 4
LOAD = 2

NAMES, SCAL_X, SCAL_PLANE = range(3)
UP_X, UP_PLANE, DOWN_PLANE, DOWN_X = 3, 8, 13, 15
STAGES = 17


def iota(shape, dim):
    return lax.broadcasted_iota(jnp.int32, shape, dim)


def one_hot(condition):
    return jnp.where(condition, 1.0, 0.0).astype(BF16)


def split(value):
    high = value.astype(BF16)
    return high, (value - high.astype(F32)).astype(BF16)


def wait_bytes(ref, sem):
    pltpu.make_async_copy(ref, ref, sem).wait()


def dot(left, right):
    return lax.dot_general(left, right, (((1,), (0,)), ((), ())), preferred_element_type=F32)


def dot_nt(left, right):
    return lax.dot_general(left, right, (((1,), (1,)), ((), ())), preferred_element_type=F32)


def kernel(
    tile_rows,
    tile_cols,
    primal_step,
    dual_step,
    tiles_hbm,
    objective,
    demand,
    primal_out,
    dual_out,
    tiles,
    flipped,
    names,
    names_in,
    row_parts,
    buf_a,
    send_b,
    recv_b,
    pay,
    rows,
    sel,
    recv_a,
    picked,
    hot_up,
    hot_down,
    scal,
    scal_x,
    scal_out,
    scal_in,
    demand8,
    tile_sem,
    send_sem,
    recv_sem,
):
    g, zh, y, x, c = (lax.axis_index(axis) for axis in AXES)
    slot_me = (zh * 4 + y) * 2 + c
    first_col = ((slot_me >> 1) * 4 + x) * 2 + c
    first_col = first_col * objective.shape[0]

    def x_device(step):
        return (g, zh, y, lax.rem(x + step, 4), c)

    def plane(step):
        og, oc, oz, oy = (step & 1, (step >> 1) & 1, (step >> 2) & 1, step >> 3)
        return (
            lax.rem(g + og, 2),
            lax.rem(zh + oz, 2),
            lax.rem(y + oy, 4),
            lax.rem(c + oc, 2),
        )

    def send(src, dst, stage, device):
        pltpu.make_async_remote_copy(
            src_ref=src,
            dst_ref=dst,
            send_sem=send_sem.at[stage],
            recv_sem=recv_sem.at[stage],
            device_id=device,
            device_id_type=MESH,
        ).start()

    barrier = pltpu.get_barrier_semaphore()
    for step in range(1, 4):
        pl.semaphore_signal(barrier, inc=1, device_id=x_device(step), device_id_type=MESH)
    for step in range(1, 32):
        pg, pz, py, pc = plane(step)
        pl.semaphore_signal(barrier, inc=1, device_id=(pg, pz, py, x, pc), device_id_type=MESH)

    def load(chunk):
        part = pl.ds(chunk * LOAD, LOAD)
        return pltpu.make_async_copy(tiles_hbm.at[part], tiles.at[part], tile_sem.at[chunk])

    for chunk in range(TILES // LOAD):
        load(chunk).start()

    sub = iota((16, 128), 0)
    lane = iota((8, 128), 1)
    down = jnp.zeros((16, 128), jnp.int32)
    along = jnp.zeros((8, 128), jnp.int32)
    for k in range(TILES):
        down = jnp.where(sub == k, tile_rows[k], down)
        along = jnp.where((lane & 15) == k, tile_rows[k], along)
    names[0:16, :] = down
    names[16:24, :] = along
    demand8[0:4, :] = demand[:, 0:128]
    demand8[4:8, :] = demand[:, 128:256]

    def column_of(k):
        return tile_cols[k] - first_col

    ones_row = jnp.ones((16, 256), BF16)
    eight = iota((8, 256), 0)
    col_total = jnp.zeros((8, 256), F32)
    for chunk in range(TILES // LOAD):
        load(chunk).wait()
        for k in range(chunk * LOAD, (chunk + 1) * LOAD):
            block = jnp.abs(tiles[k])
            row_parts[k : k + 1, :] = dot_nt(ones_row, block)[0:1]
            column = jnp.sum(block.astype(F32), axis=0, keepdims=True)
            col_total += jnp.where(eight == column_of(k), column, 0.0)

    def stage_up(q):
        high, low = split(row_parts[...])
        buf_a[q, 0, 0:16, :] = high
        buf_a[q, 0, 16:32, :] = low

    def send_up(q):
        for step in (2, 1, 3):
            send(buf_a.at[q, 0], buf_a.at[q, step], UP_X + q, x_device(step))

    row16 = iota((16, 512), 0) & 7

    def row_products(left, magnitude, turned=True, start=0, stop=TILES):
        def body(step, carry):
            for j in range(CHUNK):
                k = step * CHUNK + j
                block = flipped[k] if turned else tiles[k]
                if magnitude:
                    block = jnp.abs(block)
                sums = dot(left, block) if turned else dot_nt(left, block)
                mine = jnp.where(row16 == column_of(k), sums, 0.0)
                row_parts[pl.ds(k, 1), :] = jnp.sum(mine, axis=0, keepdims=True)
            return carry

        lax.fori_loop(start // CHUNK, stop // CHUNK, body, 0)

    eight_wide = iota((8, 512), 0)

    def column_products(magnitude):
        def body(step, total):
            lefts = []
            for j in range(CHUNK):
                k = step * CHUNK + j
                mine = eight_wide == column_of(k)
                pieces = [
                    jnp.where(mine, picked[pl.ds(kind * 16 + k, 1), :], 0.0) for kind in range(2)
                ]
                lefts.append(jnp.concatenate(pieces, axis=0).astype(BF16))
            block = tiles[pl.ds(step * CHUNK, CHUNK)].reshape(CHUNK * 512, 256)
            if magnitude:
                block = jnp.abs(block)
            return total + dot(jnp.concatenate(lefts, axis=1), block)

        return lax.fori_loop(0, TILES // CHUNK, body, jnp.zeros((16, 256), F32))

    def flip(start, stop):
        def body(step, carry):
            for j in range(2):
                k = step * 2 + j
                flipped[k] = tiles[k].T
            return carry

        lax.fori_loop(start // 2, stop // 2, body, 0)

    stage_up(0)
    col_factor = 1.0 / jnp.sqrt(col_total + EPSILON)
    rounded = jnp.concatenate([col_factor, jnp.zeros_like(col_factor)], axis=0).astype(BF16)
    row_products(rounded, True, False, 0, TILES // 2)
    pl.semaphore_wait(barrier, 34)
    for step in (2, 1, 3):
        send(names, names_in.at[step - 1], NAMES, x_device(step))
    send_up(0)
    row_products(rounded, True, False, TILES // 2, TILES)
    stage_up(1)
    send_up(1)

    flip(0, 4)
    wait_bytes(names_in, recv_sem.at[NAMES])
    lane_names = [names[16:17, :]] + [names_in[p, 16:17, :] for p in range(3)]
    down_names = [names[0:16, :]] + [names_in[p, 0:16, :] for p in range(3)]
    quarter = iota((1, 128), 1) >> 5
    narrow = lane_names[3]
    for p in range(3):
        narrow = jnp.where(quarter == p, lane_names[p], narrow)
    narrow = jnp.concatenate([narrow, narrow], axis=1)
    m = iota((128, 256), 0)
    n = iota((128, 256), 1)

    def row_id(slot, index):
        return ((((slot >> 1) * 4 + x) * 2 + (slot & 1)) * 4) + index

    hot_up[...] = one_hot(
        jnp.logical_and(narrow == row_id(m >> 3, m & 3), (n >> 7) == ((m >> 2) & 1))
    )
    n16 = iota((16, 256), 1)
    ids16 = row_id(n16 >> 4, n16 & 3)
    group = (n16 >> 2) & 3
    for p in range(4):
        named = jnp.concatenate([down_names[p], down_names[p]], axis=1) == ids16
        for half in range(2):
            for kind in range(2):
                at = p * 64 + half * 32 + kind * 16
                hot_down[at : at + 16, :] = one_hot(
                    jnp.logical_and(named, group == kind * 2 + half)
                )

    def to_owner(q):
        wait_bytes(buf_a.at[q, 1:4], recv_sem.at[UP_X + q])
        terms = buf_a[q].reshape(128, 512)
        terms = jnp.concatenate(
            [
                jnp.concatenate([terms[:, 0:128], terms[:, 256:384]], axis=1),
                jnp.concatenate([terms[:, 128:256], terms[:, 384:512]], axis=1),
            ],
            axis=0,
        )
        send_b[q] = dot(hot_up[...], terms).reshape(16, 8, 256)
        for step in range(31, 0, -1):
            pg, pz, py, pc = plane(step)
            target = (pz * 4 + py) * 2 + pc
            lanes = pl.ds(pl.multiple_of(pg * 128, 128), 128)
            send(
                send_b.at[q, target, :, lanes],
                recv_b.at[q, step - 1],
                UP_PLANE + q,
                (pg, pz, py, x, pc),
            )

    def own_total(q):
        mine = send_b[q, slot_me]
        mine = jnp.where(g == 0, mine[:, 0:128], mine[:, 128:256])
        wait_bytes(recv_b.at[q], recv_sem.at[UP_PLANE + q])
        return mine + jnp.sum(recv_b[q], axis=0)

    def to_holders(t, first, second, meanwhile):
        pay[t] = jnp.concatenate([first, second], axis=0).astype(BF16)
        for step in range(31, 0, -1):
            pg, pz, py, pc = plane(step)
            send(pay.at[t], rows.at[t, g, slot_me], DOWN_PLANE + t, (pg, pz, py, x, pc))
        pltpu.make_async_copy(
            pay.at[t], rows.at[t, g, slot_me], recv_sem.at[DOWN_PLANE + t]
        ).start()
        meanwhile()
        wait_bytes(rows.at[t], recv_sem.at[DOWN_PLANE + t])
        for half in range(2):
            chosen = dot(hot_down[...], rows[t, half].reshape(256, 128)).astype(BF16)
            for p in range(4):
                for quarter in range(2):
                    at = (half * 2 + quarter) * 128
                    begin = p * 64 + quarter * 32
                    sel[t, p, :, at : at + 128] = chosen[begin : begin + 32]
        for step in (2, 1, 3):
            send(sel.at[t, step], recv_a.at[t, step - 1], DOWN_X + t, x_device(4 - step))
        own = sel[t, 0].astype(F32)
        wait_bytes(recv_a.at[t], recv_sem.at[DOWN_X + t])
        for p in range(3):
            own = own + recv_a[t, p].astype(F32)
        picked[...] = own

    to_owner(0)
    to_owner(1)
    flip(4, 10)
    first_sum = own_total(0)
    second_sum = own_total(1)
    row_first = 1.0 / jnp.sqrt(first_sum + EPSILON)
    row_factor = row_first / jnp.sqrt(row_first * second_sum + EPSILON)
    to_holders(0, row_first, row_factor, lambda: flip(10, TILES))

    sums = column_products(True)
    col_next = col_factor / jnp.sqrt(col_factor * sums[0:8] + EPSILON)
    col_abs = col_next * sums[8:16]
    primal_rate = primal_step[0] / (col_abs + EPSILON)
    cost_scaled = col_next * objective[...]
    demand_scaled = row_factor * demand8[...]

    def squares(value):
        return jnp.sum(jnp.sum(value * value, axis=0, keepdims=True), axis=1, keepdims=True)

    scal[...] = jnp.where(iota((1, 128), 1) < 64, squares(cost_scaled), squares(demand_scaled))
    for step in (2, 1, 3):
        send(scal, scal_x.at[step - 1], SCAL_X, x_device(step))

    def high_low(value):
        top = value.astype(BF16).astype(F32)
        return jnp.concatenate([top, value - top], axis=0).astype(BF16)

    row_products(high_low(col_next), True)
    stage_up(2)
    send_up(2)
    unit = jnp.maximum(-primal_rate * cost_scaled, 0.0)
    row_products(high_low(col_next * (2.0 * unit)), False)
    stage_up(3)
    send_up(3)

    wait_bytes(scal_x, recv_sem.at[SCAL_X])
    scal_out[...] = scal[...] + scal_x[0] + scal_x[1] + scal_x[2]
    for step in range(31, 0, -1):
        pg, pz, py, pc = plane(step)
        send(scal_out, scal_in.at[step - 1], SCAL_PLANE, (pg, pz, py, x, pc))
    to_owner(2)
    to_owner(3)
    wait_bytes(scal_in, recv_sem.at[SCAL_PLANE])
    both_squares = scal_out[...] + jnp.sum(scal_in[...], axis=0)
    wide_count = 64
    cost_gain = 1.0 / jnp.sqrt(both_squares[:, 0:1] / (8 * wide_count * 512) + EPSILON)
    demand_gain = 1.0 / jnp.sqrt(both_squares[:, 64:65] / (4 * wide_count * 512) + EPSILON)
    primal = cost_gain * unit
    cost_hat = cost_scaled * cost_gain
    demand_hat = demand_scaled * demand_gain

    dual_rate = dual_step[0] / (row_factor * own_total(2) + EPSILON)
    dual = dual_rate * (demand_hat - row_factor * (own_total(3) * cost_gain))
    weighted = row_factor * dual.astype(BF16).astype(F32)
    top = weighted.astype(BF16).astype(F32)
    to_holders(1, top, weighted - top, lambda: None)

    sums = column_products(False)
    pulled = col_next * (sums[0:8] + sums[8:16])
    primal_next = jnp.maximum(primal - primal_rate * (cost_hat - pulled), 0.0)
    primal_out[...] = primal_next
    bar = (2.0 * primal_next - primal).astype(BF16).astype(F32)
    row_products(high_low(col_next * bar), False)
    stage_up(4)
    send_up(4)
    to_owner(4)
    dual_next = dual + dual_rate * (demand_hat - row_factor * own_total(4))
    dual_out[:, 0:128] = dual_next[0:4]
    dual_out[:, 128:256] = dual_next[4:8]

    wait_bytes(names_in, send_sem.at[NAMES])
    wait_bytes(scal_x, send_sem.at[SCAL_X])
    wait_bytes(scal_in, send_sem.at[SCAL_PLANE])
    for q in range(5):
        wait_bytes(buf_a.at[q, 1:4], send_sem.at[UP_X + q])
        wait_bytes(recv_b.at[q], send_sem.at[UP_PLANE + q])
    for t in range(2):
        wait_bytes(recv_b.at[t], send_sem.at[DOWN_PLANE + t])
        wait_bytes(recv_a.at[t], send_sem.at[DOWN_X + t])


def hand_over(primal, dual, primal_out, dual_out):
    primal_out[...] = primal[...]
    dual_out[...] = dual[...]


def on_device(tile_values, tile_rows, tile_cols, objective, demand, primal_step, dual_step):
    vmem = pl.BlockSpec(memory_space=pltpu.VMEM)
    smem = pl.BlockSpec(memory_space=pltpu.SMEM)
    shapes = (
        jax.ShapeDtypeStruct(objective.shape, F32),
        jax.ShapeDtypeStruct(demand.shape, F32),
    )
    results = pl.pallas_call(
        kernel,
        out_shape=shapes,
        in_specs=[smem, smem, smem, smem, pl.BlockSpec(memory_space=pl.ANY), vmem, vmem],
        out_specs=(vmem, vmem),
        scratch_shapes=[
            pltpu.VMEM((TILES, 512, 256), BF16),
            pltpu.VMEM((TILES, 256, 512), BF16),
            pltpu.VMEM((24, 128), jnp.int32),
            pltpu.VMEM((3, 24, 128), jnp.int32),
            pltpu.VMEM((16, 512), F32),
            pltpu.VMEM((5, 4, 32, 512), BF16),
            pltpu.VMEM((5, 16, 8, 256), F32),
            pltpu.VMEM((5, 31, 8, 128), F32),
            pltpu.VMEM((2, 16, 128), BF16),
            pltpu.VMEM((2, 2, 16, 16, 128), BF16),
            pltpu.VMEM((2, 4, 32, 512), BF16),
            pltpu.VMEM((2, 3, 32, 512), BF16),
            pltpu.VMEM((32, 512), F32),
            pltpu.VMEM((128, 256), BF16),
            pltpu.VMEM((256, 256), BF16),
            pltpu.VMEM((1, 128), F32),
            pltpu.VMEM((3, 1, 128), F32),
            pltpu.VMEM((1, 128), F32),
            pltpu.VMEM((31, 1, 128), F32),
            pltpu.VMEM((8, 128), F32),
            pltpu.SemaphoreType.DMA((TILES // LOAD,)),
            pltpu.SemaphoreType.DMA((STAGES,)),
            pltpu.SemaphoreType.DMA((STAGES,)),
        ],
        compiler_params=pltpu.CompilerParams(collective_id=0, has_side_effects=True),
    )(
        tile_rows,
        tile_cols,
        primal_step.reshape(1),
        dual_step.reshape(1),
        tile_values,
        objective,
        demand,
    )
    return pl.pallas_call(
        hand_over, out_shape=shapes, in_specs=[vmem, vmem], out_specs=(vmem, vmem)
    )(*results)


def solution(mesh):
    devices = mesh.devices.reshape(mesh.shape["grp"], 2, 4, 4, 2)
    return jax.shard_map(
        on_device,
        mesh=Mesh(devices, AXES),
        in_specs=(P(WIDE, None, "grp"), P(WIDE), P(WIDE), P(WIDE, "grp"), P(WIDE, "grp"), P(), P()),
        out_specs=(P(WIDE, "grp"), P(WIDE, "grp")),
        check_vma=False,
    )
```

time: 75 us -> 67.4 us (0.90)
  Pallas kernels: 68.4 us -> 64.5 us
  local copies, waits for them, and re-layouts: 2.56 us -> 0 us
  other arithmetic: 1.17 us -> 0 us
    pallas_call x1 -> x2, Pallas kernels: 68.4 us -> 64.5 us  [the longest x1 63.2 us: on_device(): pl.pallas_call(kernel, out_shape=shapes, in_specs=[smem, smem, smem, smem...]
    unnamed x2 -> x0, local copies, waits for them, and re-layouts: 2.56 us -> none
    sub x1 -> x0, other arithmetic: 1.17 us -> none  [on_device(): tile_cols - wide_index * objective.shape[0]]
where the time goes in v2:
time: 67.4 us; the launch traced here: 66.4 us
  Pallas kernels  64.5 us (96%)
  between operations  1.93 us (3%)
    pallas_call x1, Pallas kernels, on_device(): pl.pallas_call(kernel, out_shape=shapes, in_specs=[smem, smem, smem, smem...  63.2 us

profile of v2, /device:TPU:0, one launch (start us, length us, event | category | flops | bytes accessed | tf_op | source)
XLA Modules:
  0.0 66.4 jit_solution(3192203573719750787)
XLA Ops:
  1.9 63.2 %shard_map.86 = (f32[8,256]{1,0:T(8,128)}, f32[4,256]{1,0:T(4,128)}) custom-call(s32[16]{0:T(128)} %tile_rows.1, s32[16]{0:T(128)} %tile_cols.1, f32[1]{0:T(128)} %bitcast.2.primal_step, f32[1]{0:T(128)} %bitcast.3.dual_step, bf16[16,512,256]{2,1,0:T(8,128)(2,1)} %tiles_hbm.1, f32[8,256]{1,0:T(8,128)} %objective.1, f32[4,256]{1,0:T(4,128)} %demand.1), custom_call_target="tpu_custom_call" | custom-call | tf_op jit(solution)/shard_map/pallas_call | solution.py:393
  65.1 1.3 %shard_map.87 = (f32[8,256]{1,0:T(8,128)}, f32[4,256]{1,0:T(4,128)}) custom-call(f32[8,256]{1,0:T(8,128)} %get-tuple-element.4.primal, f32[4,256]{1,0:T(4,128)} %get-tuple-element.5.dual), custom_call_target="tpu_custom_call" | custom-call | tf_op jit(solution)/shard_map/pallas_call | solution.py:433

commit v3 on v2

v3 whole, which is shorter than its diff:
```python
import functools

import jax
import jax.numpy as jnp
from jax import lax
from jax.experimental import pallas as pl
from jax.experimental.pallas import tpu as pltpu
from jax.sharding import Mesh
from jax.sharding import PartitionSpec as P

AXES = ("grp", "zh", "y", "x", "core")
WIDE = AXES[1:]
EPSILON = 1e-06
MESH = pl.DeviceIdType.MESH
F32 = jnp.float32
BF16 = jnp.bfloat16
TILES = 16
CHUNK = 4
LOAD = 2

NAMES, SCAL_X, SCAL_PLANE = range(3)
UP_X, UP_PLANE = 3, 6
UP_CORE, UP_ALL, DOWN_ALL, DOWN_CORE = 9, 11, 13, 15
STAGES = 17


def offsets():
    found = []
    for og in range(2):
        for oz in range(2):
            for oy in range(4):
                for ox in range(4):
                    hops = (1 if og else 2 * oz) + min(oy, 4 - oy) + min(ox, 4 - ox)
                    found.append((hops, og, oz, oy, ox))
    return [entry[1:] for entry in sorted(found, reverse=True) if entry[0]]


CHIPS = offsets()
PLANE = [(og, oz, oy, oc) for og, oz, oy, ox in CHIPS if ox == 0 for oc in range(2)]
PLANE.append((0, 0, 0, 1))


def iota(shape, dim):
    return lax.broadcasted_iota(jnp.int32, shape, dim)


def one_hot(condition):
    return jnp.where(condition, 1.0, 0.0).astype(BF16)


def split(value):
    high = value.astype(BF16)
    return high, (value - high.astype(F32)).astype(BF16)


def wait_bytes(ref, sem):
    pltpu.make_async_copy(ref, ref, sem).wait()


def dot(left, right):
    return lax.dot_general(left, right, (((1,), (0,)), ((), ())), preferred_element_type=F32)


def dot_nt(left, right):
    return lax.dot_general(left, right, (((1,), (1,)), ((), ())), preferred_element_type=F32)


def kernel(
    rows_hbm,
    cols_hbm,
    primal_step,
    dual_step,
    tiles_hbm,
    objective_hbm,
    demand_hbm,
    primal_out,
    dual_out,
    tile_rows,
    tile_cols,
    objective,
    demand,
    tiles,
    flipped,
    names,
    names_in,
    row_parts,
    col_parts,
    buf_a,
    send_b,
    recv_b,
    buf_c,
    send_c,
    recv_c,
    pay,
    rows,
    sel,
    recv_a,
    picked,
    hot_up,
    hot_core,
    hot_down,
    scal,
    scal_x,
    scal_out,
    scal_in,
    demand8,
    tile_sem,
    small_sem,
    send_sem,
    recv_sem,
):
    g, zh, y, x, c = (lax.axis_index(axis) for axis in AXES)
    slot_me = (zh * 4 + y) * 2 + c
    first_col = ((slot_me >> 1) * 4 + x) * 2 + c
    first_col = first_col * objective.shape[0]

    def x_device(step):
        return (g, zh, y, lax.rem(x + step, 4), c)

    def plane(entry):
        og, oz, oy, oc = entry
        return (
            lax.rem(g + og, 2),
            lax.rem(zh + oz, 2),
            lax.rem(y + oy, 4),
            lax.rem(c + oc, 2),
        )

    def chip(entry):
        og, oz, oy, ox = entry
        return (
            lax.rem(g + og, 2),
            lax.rem(zh + oz, 2),
            lax.rem(y + oy, 4),
            lax.rem(x + ox, 4),
        )

    other_core = (g, zh, y, x, 1 - c)
    chip_me = (zh * 4 + y) * 4 + x

    def send(src, dst, stage, device):
        pltpu.make_async_remote_copy(
            src_ref=src,
            dst_ref=dst,
            send_sem=send_sem.at[stage],
            recv_sem=recv_sem.at[stage],
            device_id=device,
            device_id_type=MESH,
        ).start()

    small = [
        pltpu.make_async_copy(src, dst, small_sem.at[i])
        for i, (src, dst) in enumerate(
            (
                (cols_hbm, tile_cols),
                (rows_hbm, tile_rows),
                (demand_hbm, demand),
                (objective_hbm, objective),
            )
        )
    ]
    for copy in small:
        copy.start()

    def load(chunk):
        part = pl.ds(chunk * LOAD, LOAD)
        return pltpu.make_async_copy(tiles_hbm.at[part], tiles.at[part], tile_sem.at[chunk])

    for chunk in range(TILES // LOAD):
        load(chunk).start()

    barrier = pltpu.get_barrier_semaphore()
    for step in range(1, 4):
        pl.semaphore_signal(barrier, inc=1, device_id=x_device(step), device_id_type=MESH)
    for entry in PLANE:
        pg, pz, py, pc = plane(entry)
        pl.semaphore_signal(barrier, inc=1, device_id=(pg, pz, py, x, pc), device_id_type=MESH)

    def column_of(k):
        return tile_cols[k] - first_col

    ones_row = jnp.ones((16, 256), BF16)
    for chunk in range(TILES // LOAD):
        load(chunk).wait()
        for k in range(chunk * LOAD, (chunk + 1) * LOAD):
            block = tiles[k]
            turned = block.T
            flipped[k] = turned
            row_parts[k : k + 1, :] = dot(ones_row, jnp.abs(turned))[0:1]
            col_parts[k : k + 1, :] = jnp.sum(
                jnp.abs(block).astype(F32), axis=0, keepdims=True
            )

    for copy in small:
        copy.wait()

    sub = iota((16, 128), 0)
    lane = iota((8, 128), 1)
    down = jnp.zeros((16, 128), jnp.int32)
    along = jnp.zeros((8, 128), jnp.int32)
    for k in range(TILES):
        down = jnp.where(sub == k, tile_rows[k], down)
        along = jnp.where((lane & 15) == k, tile_rows[k], along)
    names[0:16, :] = down
    names[16:24, :] = along
    demand8[0:4, :] = demand[:, 0:128]
    demand8[4:8, :] = demand[:, 128:256]

    eight = iota((8, 256), 0)
    col_total = jnp.zeros((8, 256), F32)
    for k in range(TILES):
        col_total += jnp.where(eight == column_of(k), col_parts[k : k + 1, :], 0.0)

    def stage_up(buf):
        high, low = split(row_parts[...])
        buf[0, 0:16, :] = high
        buf[0, 16:32, :] = low

    def send_up(q):
        for step in (2, 1, 3):
            send(buf_a.at[q, 0], buf_a.at[q, step], UP_X + q, x_device(step))

    def send_core(t):
        send(buf_c.at[t, 0], buf_c.at[t, 1], UP_CORE + t, other_core)

    row16 = iota((16, 512), 0) & 7

    def row_products(left, magnitude):
        def body(step, carry):
            for j in range(CHUNK):
                k = step * CHUNK + j
                block = flipped[k]
                if magnitude:
                    block = jnp.abs(block)
                mine = jnp.where(row16 == column_of(k), dot(left, block), 0.0)
                row_parts[pl.ds(k, 1), :] = jnp.sum(mine, axis=0, keepdims=True)
            return carry

        lax.fori_loop(0, TILES // CHUNK, body, 0)

    eight_wide = iota((8, 512), 0)

    def column_products(magnitude):
        def body(step, total):
            lefts = []
            for j in range(CHUNK):
                k = step * CHUNK + j
                mine = eight_wide == column_of(k)
                pieces = [
                    jnp.where(mine, picked[pl.ds(kind * 16 + k, 1), :], 0.0) for kind in range(2)
                ]
                lefts.append(jnp.concatenate(pieces, axis=0).astype(BF16))
            block = tiles[pl.ds(step * CHUNK, CHUNK)].reshape(CHUNK * 512, 256)
            if magnitude:
                block = jnp.abs(block)
            return total + dot(jnp.concatenate(lefts, axis=1), block)

        return lax.fori_loop(0, TILES // CHUNK, body, jnp.zeros((16, 256), F32))

    stage_up(buf_a.at[0])
    col_factor = 1.0 / jnp.sqrt(col_total + EPSILON)
    rounded = jnp.concatenate([col_factor, jnp.zeros_like(col_factor)], axis=0).astype(BF16)
    row_products(rounded, True)
    stage_up(buf_a.at[1])
    pl.semaphore_wait(barrier, 34)
    for step in (2, 1, 3):
        send(names, names_in.at[step - 1], NAMES, x_device(step))
    send(names, names_in.at[3], NAMES, other_core)
    send_up(0)
    send_up(1)

    wait_bytes(names_in, recv_sem.at[NAMES])
    lane_names = [names[16:17, :]] + [names_in[p, 16:17, :] for p in range(3)]
    quarter = iota((1, 128), 1) >> 5
    narrow = lane_names[3]
    for p in range(3):
        narrow = jnp.where(quarter == p, lane_names[p], narrow)
    narrow = jnp.concatenate([narrow, narrow], axis=1)
    m = iota((128, 256), 0)
    n = iota((128, 256), 1)

    def row_id(slot, index):
        return ((((slot >> 1) * 4 + x) * 2 + (slot & 1)) * 4) + index

    hot_up[...] = one_hot(
        jnp.logical_and(narrow == row_id(m >> 3, m & 3), (n >> 7) == ((m >> 2) & 1))
    )
    core_names = jnp.where(
        ((iota((1, 128), 1) >> 5) & 1) == 0, lane_names[0], names_in[3, 16:17, :]
    )
    m = iota((256, 128), 0)
    n = iota((256, 128), 1)

    def core_id(slot, index):
        return (slot * 2 + c) * 4 + index

    hot_core[...] = one_hot(
        jnp.logical_and(core_names == core_id(m >> 3, m & 3), (n >> 6) == ((m >> 2) & 1))
    )
    n16 = iota((16, 512), 1)
    ids16 = core_id(n16 >> 4, n16 & 3)
    group = (n16 >> 2) & 3
    for p, held in enumerate((names[0:16, :], names_in[3, 0:16, :])):
        named = jnp.concatenate([held] * 4, axis=1) == ids16
        for half in range(2):
            for kind in range(2):
                at = p * 64 + half * 32 + kind * 16
                hot_down[at : at + 16, :] = one_hot(
                    jnp.logical_and(named, group == kind * 2 + half)
                )

    def by_quarters(terms):
        return jnp.concatenate(
            [
                jnp.concatenate([terms[:, 0:128], terms[:, 256:384]], axis=1),
                jnp.concatenate([terms[:, 128:256], terms[:, 384:512]], axis=1),
            ],
            axis=0,
        )

    def to_owner(q):
        wait_bytes(buf_a.at[q, 1:4], recv_sem.at[UP_X + q])
        terms = by_quarters(buf_a[q].reshape(128, 512))
        send_b[q] = dot(hot_up[...], terms).reshape(16, 8, 256)
        for index, entry in enumerate(PLANE):
            pg, pz, py, pc = plane(entry)
            target = (pz * 4 + py) * 2 + pc
            lanes = pl.ds(pl.multiple_of(pg * 128, 128), 128)
            send(
                send_b.at[q, target, :, lanes],
                recv_b.at[q, index],
                UP_PLANE + q,
                (pg, pz, py, x, pc),
            )

    def own_total(q):
        mine = send_b[q, slot_me]
        mine = jnp.where(g == 0, mine[:, 0:128], mine[:, 128:256])
        wait_bytes(recv_b.at[q], recv_sem.at[UP_PLANE + q])
        return mine + jnp.sum(recv_b[q], axis=0)

    def to_owner_direct(t):
        wait_bytes(buf_c.at[t, 1], recv_sem.at[UP_CORE + t])
        terms = by_quarters(buf_c[t].reshape(64, 512))
        send_c[t] = dot(hot_core[...], terms).reshape(32, 8, 256)
        for index, entry in enumerate(CHIPS):
            pg, pz, py, px = chip(entry)
            target = (pz * 4 + py) * 4 + px
            lanes = pl.ds(pl.multiple_of(pg * 128, 128), 128)
            send(
                send_c.at[t, target, :, lanes],
                recv_c.at[t, index],
                UP_ALL + t,
                (pg, pz, py, px, c),
            )

    def own_total_direct(t):
        mine = send_c[t, chip_me]
        mine = jnp.where(g == 0, mine[:, 0:128], mine[:, 128:256])
        wait_bytes(recv_c.at[t], recv_sem.at[UP_ALL + t])
        return mine + jnp.sum(recv_c[t], axis=0)

    def to_holders(t, first, second):
        pay[t] = jnp.concatenate([first, second], axis=0).astype(BF16)
        for entry in CHIPS:
            pg, pz, py, px = chip(entry)
            send(pay.at[t], rows.at[t, g, chip_me], DOWN_ALL + t, (pg, pz, py, px, c))
        pltpu.make_async_copy(
            pay.at[t], rows.at[t, g, chip_me], recv_sem.at[DOWN_ALL + t]
        ).start()
        wait_bytes(rows.at[t], recv_sem.at[DOWN_ALL + t])
        for half in range(2):
            chosen = dot(hot_down[...], rows[t, half].reshape(512, 128)).astype(BF16)
            for p in range(2):
                for quarter in range(2):
                    at = (half * 2 + quarter) * 128
                    begin = p * 64 + quarter * 32
                    sel[t, p, :, at : at + 128] = chosen[begin : begin + 32]
        send(sel.at[t, 1], recv_a.at[t], DOWN_CORE + t, other_core)
        own = sel[t, 0].astype(F32)
        wait_bytes(recv_a.at[t], recv_sem.at[DOWN_CORE + t])
        picked[...] = own + recv_a[t].astype(F32)

    to_owner(0)
    to_owner(1)
    first_sum = own_total(0)
    second_sum = own_total(1)
    row_first = 1.0 / jnp.sqrt(first_sum + EPSILON)
    row_factor = row_first / jnp.sqrt(row_first * second_sum + EPSILON)
    to_holders(0, row_first, row_factor)

    sums = column_products(True)
    col_next = col_factor / jnp.sqrt(col_factor * sums[0:8] + EPSILON)
    col_abs = col_next * sums[8:16]
    primal_rate = primal_step[()] / (col_abs + EPSILON)
    cost_scaled = col_next * objective[...]
    demand_scaled = row_factor * demand8[...]

    def squares(value):
        return jnp.sum(jnp.sum(value * value, axis=0, keepdims=True), axis=1, keepdims=True)

    scal[...] = jnp.where(iota((1, 128), 1) < 64, squares(cost_scaled), squares(demand_scaled))
    for step in (2, 1, 3):
        send(scal, scal_x.at[step - 1], SCAL_X, x_device(step))

    def high_low(value):
        top = value.astype(BF16).astype(F32)
        return jnp.concatenate([top, value - top], axis=0).astype(BF16)

    row_products(high_low(col_next), True)
    stage_up(buf_a.at[2])
    send_up(2)
    unit = jnp.maximum(-primal_rate * cost_scaled, 0.0)
    row_products(high_low(col_next * (2.0 * unit)), False)
    stage_up(buf_c.at[0])
    send_core(0)

    wait_bytes(scal_x, recv_sem.at[SCAL_X])
    scal_out[...] = scal[...] + scal_x[0] + scal_x[1] + scal_x[2]
    for index, entry in enumerate(PLANE):
        pg, pz, py, pc = plane(entry)
        send(scal_out, scal_in.at[index], SCAL_PLANE, (pg, pz, py, x, pc))
    to_owner_direct(0)
    to_owner(2)
    wait_bytes(scal_in, recv_sem.at[SCAL_PLANE])
    both_squares = scal_out[...] + jnp.sum(scal_in[...], axis=0)
    wide_count = 64
    cost_gain = 1.0 / jnp.sqrt(both_squares[:, 0:1] / (8 * wide_count * 512) + EPSILON)
    demand_gain = 1.0 / jnp.sqrt(both_squares[:, 64:65] / (4 * wide_count * 512) + EPSILON)
    primal = cost_gain * unit
    cost_hat = cost_scaled * cost_gain
    demand_hat = demand_scaled * demand_gain

    dual_rate = dual_step[()] / (row_factor * own_total(2) + EPSILON)
    dual = dual_rate * (demand_hat - row_factor * (own_total_direct(0) * cost_gain))
    weighted = row_factor * dual.astype(BF16).astype(F32)
    top = weighted.astype(BF16).astype(F32)
    to_holders(1, top, weighted - top)

    sums = column_products(False)
    pulled = col_next * (sums[0:8] + sums[8:16])
    primal_next = jnp.maximum(primal - primal_rate * (cost_hat - pulled), 0.0)
    primal_out[...] = primal_next
    bar = (2.0 * primal_next - primal).astype(BF16).astype(F32)
    row_products(high_low(col_next * bar), False)
    stage_up(buf_c.at[1])
    send_core(1)
    to_owner_direct(1)
    dual_next = dual + dual_rate * (demand_hat - row_factor * own_total_direct(1))
    dual_out[:, 0:128] = dual_next[0:4]
    dual_out[:, 128:256] = dual_next[4:8]

    wait_bytes(names_in, send_sem.at[NAMES])
    wait_bytes(scal_x, send_sem.at[SCAL_X])
    wait_bytes(scal_in, send_sem.at[SCAL_PLANE])
    for q in range(3):
        wait_bytes(buf_a.at[q, 1:4], send_sem.at[UP_X + q])
        wait_bytes(recv_b.at[q], send_sem.at[UP_PLANE + q])
    for t in range(2):
        wait_bytes(buf_c.at[t, 1], send_sem.at[UP_CORE + t])
        wait_bytes(recv_c.at[t], send_sem.at[UP_ALL + t])
        wait_bytes(recv_c.at[t], send_sem.at[DOWN_ALL + t])
        wait_bytes(recv_a.at[t], send_sem.at[DOWN_CORE + t])


def hand_over(primal, dual, primal_out, dual_out):
    primal_out[...] = primal[...]
    dual_out[...] = dual[...]


def on_device(tile_values, tile_rows, tile_cols, objective, demand, primal_step, dual_step):
    vmem = pl.BlockSpec(memory_space=pltpu.VMEM)
    hbm = pl.BlockSpec(memory_space=pl.ANY)
    smem = pl.BlockSpec(memory_space=pltpu.SMEM)
    shapes = (
        jax.ShapeDtypeStruct(objective.shape, F32),
        jax.ShapeDtypeStruct(demand.shape, F32),
    )
    results = pl.pallas_call(
        kernel,
        out_shape=tuple(pltpu.VMEM(shape.shape, F32) for shape in shapes),
        in_specs=[hbm, hbm, smem, smem, hbm, hbm, hbm],
        out_specs=(vmem, vmem),
        scratch_shapes=[
            pltpu.SMEM(tile_rows.shape, jnp.int32),
            pltpu.SMEM(tile_cols.shape, jnp.int32),
            pltpu.VMEM(objective.shape, F32),
            pltpu.VMEM(demand.shape, F32),
            pltpu.VMEM((TILES, 512, 256), BF16),
            pltpu.VMEM((TILES, 256, 512), BF16),
            pltpu.VMEM((24, 128), jnp.int32),
            pltpu.VMEM((4, 24, 128), jnp.int32),
            pltpu.VMEM((16, 512), F32),
            pltpu.VMEM((16, 256), F32),
            pltpu.VMEM((3, 4, 32, 512), BF16),
            pltpu.VMEM((3, 16, 8, 256), F32),
            pltpu.VMEM((3, 31, 8, 128), F32),
            pltpu.VMEM((2, 2, 32, 512), BF16),
            pltpu.VMEM((2, 32, 8, 256), F32),
            pltpu.VMEM((2, 63, 8, 128), F32),
            pltpu.VMEM((2, 16, 128), BF16),
            pltpu.VMEM((2, 2, 32, 16, 128), BF16),
            pltpu.VMEM((2, 2, 32, 512), BF16),
            pltpu.VMEM((2, 32, 512), BF16),
            pltpu.VMEM((32, 512), F32),
            pltpu.VMEM((128, 256), BF16),
            pltpu.VMEM((256, 128), BF16),
            pltpu.VMEM((128, 512), BF16),
            pltpu.VMEM((1, 128), F32),
            pltpu.VMEM((3, 1, 128), F32),
            pltpu.VMEM((1, 128), F32),
            pltpu.VMEM((31, 1, 128), F32),
            pltpu.VMEM((8, 128), F32),
            pltpu.SemaphoreType.DMA((TILES // LOAD,)),
            pltpu.SemaphoreType.DMA((4,)),
            pltpu.SemaphoreType.DMA((STAGES,)),
            pltpu.SemaphoreType.DMA((STAGES,)),
        ],
        compiler_params=pltpu.CompilerParams(collective_id=0, has_side_effects=True),
    )(
        tile_rows,
        tile_cols,
        primal_step,
        dual_step,
        tile_values,
        objective,
        demand,
    )
    results = [pltpu.with_memory_space_constraint(r, pltpu.VMEM) for r in results]
    return pl.pallas_call(
        hand_over, out_shape=shapes, in_specs=[vmem, vmem], out_specs=(vmem, vmem)
    )(*results)


def solution(mesh):
    devices = mesh.devices.reshape(mesh.shape["grp"], 2, 4, 4, 2)
    return jax.shard_map(
        on_device,
        mesh=Mesh(devices, AXES),
        in_specs=(P(WIDE, None, "grp"), P(WIDE), P(WIDE), P(WIDE, "grp"), P(WIDE, "grp"), P(), P()),
        out_specs=(P(WIDE, "grp"), P(WIDE, "grp")),
        check_vma=False,
    )
```

time: 67.4 us -> 59.7 us (0.89); the launches traced: 66.4 us -> 59.6 us
  Pallas kernels: 64.5 us -> 57.6 us
    pallas_call x1, Pallas kernels: 63.2 us -> 57 us  [on_device(): pl.pallas_call(kernel, out_shape=tuple((pltpu.VMEM(shape.shape, F32) for...]
    pallas_call x1, Pallas kernels: 1.3 us -> 0.6 us  [on_device(): pl.pallas_call(hand_over, out_shape=shapes, in_specs=[vmem, vmem], out_sp...]
where the time goes in v3:
time: 59.7 us; the launch traced here: 59.6 us
  Pallas kernels  57.6 us (96%)
  between operations  1.93 us (3%)
    pallas_call x1, Pallas kernels, on_device(): pl.pallas_call(kernel, out_shape=tuple((pltpu.VMEM(shape.shape, F32) for...  57 us

profile of v3, /device:TPU:0, one launch (start us, length us, event | category | flops | bytes accessed | tf_op | source)
XLA Modules:
  0.0 59.6 jit_solution(7761469926758504463)
XLA Ops:
  1.9 57.0 %shard_map.86 = (f32[8,256]{1,0:T(8,128)S(1)}, f32[4,256]{1,0:T(4,128)S(1)}) custom-call(s32[16]{0:T(128)} %rows_hbm.1, s32[16]{0:T(128)} %cols_hbm.1, f32[]{:T(128)S(6)} %copy.9.primal_step, f32[]{:T(128)S(6)} %copy.10.dual_step, bf16[16,512,256]{2,1,0:T(8,128)(2,1)} %tiles_hbm.1, f32[8,256]{1,0:T(8,128)} %objective_hbm.1, f32[4,256]{1,0:T(4,128)} %demand_hbm.1), custom_call_target="tpu_custom_call" | custom-call | tf_op jit(solution)/shard_map/pallas_call | solution.py:479
  59.0 0.6 %shard_map.87 = (f32[8,256]{1,0:T(8,128)}, f32[4,256]{1,0:T(4,128)}) custom-call(f32[8,256]{1,0:T(8,128)S(1)} %get-tuple-element.4.primal, f32[4,256]{1,0:T(4,128)S(1)} %get-tuple-element.5.dual), custom_call_target="tpu_custom_call" | custom-call | tf_op jit(solution)/shard_map/pallas_call | solution.py:530

commit v4 on v3

--- a/solution.py
+++ b/solution.py
@@ -17,11 +17,12 @@
 TILES = 16
 CHUNK = 4
 LOAD = 2
-
-NAMES, SCAL_X, SCAL_PLANE = range(3)
-UP_X, UP_PLANE = 3, 6
-UP_CORE, UP_ALL, DOWN_ALL, DOWN_CORE = 9, 11, 13, 15
-STAGES = 17
+EARLY = 8
+
+NAMES, NAMES_CORE, SCAL_X, SCAL_PLANE = range(4)
+UP_X, UP_PLANE = 4, 6
+UP_CORE, UP_ALL, DOWN_ALL, DOWN_CORE = 8, 11, 14, 16
+STAGES = 18
 
 
 def offsets():
@@ -83,7 +84,10 @@
     flipped,
     names,
     names_in,
+    along_out,
+    along_in,
     row_parts,
+    first_parts,
     col_parts,
     buf_a,
     send_b,
@@ -106,6 +110,7 @@
     demand8,
     tile_sem,
     small_sem,
+    entered,
     send_sem,
     recv_sem,
 ):
@@ -179,14 +184,12 @@
     def column_of(k):
         return tile_cols[k] - first_col
 
-    ones_row = jnp.ones((16, 256), BF16)
     for chunk in range(TILES // LOAD):
         load(chunk).wait()
         for k in range(chunk * LOAD, (chunk + 1) * LOAD):
             block = tiles[k]
-            turned = block.T
-            flipped[k] = turned
-            row_parts[k : k + 1, :] = dot(ones_row, jnp.abs(turned))[0:1]
+            if k < EARLY:
+                flipped[k] = block.T
             col_parts[k : k + 1, :] = jnp.sum(
                 jnp.abs(block).astype(F32), axis=0, keepdims=True
             )
@@ -203,6 +206,7 @@
         along = jnp.where((lane & 15) == k, tile_rows[k], along)
     names[0:16, :] = down
     names[16:24, :] = along
+    along_out[...] = along[0:1]
     demand8[0:4, :] = demand[:, 0:128]
     demand8[4:8, :] = demand[:, 128:256]
 
@@ -211,8 +215,8 @@
     for k in range(TILES):
         col_total += jnp.where(eight == column_of(k), col_parts[k : k + 1, :], 0.0)
 
-    def stage_up(buf):
-        high, low = split(row_parts[...])
+    def stage_up(buf, parts):
+        high, low = split(parts[...])
         buf[0, 0:16, :] = high
         buf[0, 16:32, :] = low
 
@@ -237,8 +241,6 @@
             return carry
 
         lax.fori_loop(0, TILES // CHUNK, body, 0)
-
-    eight_wide = iota((8, 512), 0)
 
     def column_products(magnitude):
         def body(step, total):
@@ -257,57 +259,72 @@
 
         return lax.fori_loop(0, TILES // CHUNK, body, jnp.zeros((16, 256), F32))
 
-    stage_up(buf_a.at[0])
     col_factor = 1.0 / jnp.sqrt(col_total + EPSILON)
-    rounded = jnp.concatenate([col_factor, jnp.zeros_like(col_factor)], axis=0).astype(BF16)
-    row_products(rounded, True)
-    stage_up(buf_a.at[1])
+    left = jnp.concatenate([col_factor, jnp.where(eight == 0, 1.0, 0.0)], axis=0).astype(BF16)
+    eight_wide = iota((8, 512), 0)
+
+    def both_sums(turned, step, carry):
+        for j in range(CHUNK):
+            k = step * CHUNK + j
+            if turned:
+                sums = dot(left, jnp.abs(flipped[k]))
+            else:
+                sums = dot_nt(left, jnp.abs(tiles[k]))
+            mine = jnp.where(eight_wide == column_of(k), sums[0:8], 0.0)
+            row_parts[pl.ds(k, 1), :] = jnp.sum(mine, axis=0, keepdims=True)
+            first_parts[pl.ds(k, 1), :] = sums[8:9]
+        return carry
+
+    lax.fori_loop(0, EARLY // CHUNK, functools.partial(both_sums, True), 0)
+    lax.fori_loop(EARLY // CHUNK, TILES // CHUNK, functools.partial(both_sums, False), 0)
+    stage_up(buf_c.at[0], row_parts)
+    stage_up(buf_a.at[0], first_parts)
     pl.semaphore_wait(barrier, 34)
     for step in (2, 1, 3):
-        send(names, names_in.at[step - 1], NAMES, x_device(step))
-    send(names, names_in.at[3], NAMES, other_core)
+        pl.semaphore_signal(entered, inc=1, device_id=x_device(step), device_id_type=MESH)
+    send(names, names_in, NAMES_CORE, other_core)
+    send_core(0)
     send_up(0)
-    send_up(1)
-
-    wait_bytes(names_in, recv_sem.at[NAMES])
-    lane_names = [names[16:17, :]] + [names_in[p, 16:17, :] for p in range(3)]
-    quarter = iota((1, 128), 1) >> 5
-    narrow = lane_names[3]
-    for p in range(3):
-        narrow = jnp.where(quarter == p, lane_names[p], narrow)
-    narrow = jnp.concatenate([narrow, narrow], axis=1)
-    m = iota((128, 256), 0)
-    n = iota((128, 256), 1)
-
-    def row_id(slot, index):
-        return ((((slot >> 1) * 4 + x) * 2 + (slot & 1)) * 4) + index
-
-    hot_up[...] = one_hot(
-        jnp.logical_and(narrow == row_id(m >> 3, m & 3), (n >> 7) == ((m >> 2) & 1))
-    )
-    core_names = jnp.where(
-        ((iota((1, 128), 1) >> 5) & 1) == 0, lane_names[0], names_in[3, 16:17, :]
-    )
-    m = iota((256, 128), 0)
-    n = iota((256, 128), 1)
+    for step in (2, 1, 3):
+        send(along_out, along_in.at[step - 1], NAMES, x_device(step))
+
+    def core_tables():
+        core_names = jnp.where(
+            ((iota((1, 128), 1) >> 5) & 1) == 0, names[16:17, :], names_in[16:17, :]
+        )
+        m = iota((256, 128), 0)
+        n = iota((256, 128), 1)
+        hot_core[...] = one_hot(
+            jnp.logical_and(core_names == core_id(m >> 3, m & 3), (n >> 6) == ((m >> 2) & 1))
+        )
 
     def core_id(slot, index):
         return (slot * 2 + c) * 4 + index
 
-    hot_core[...] = one_hot(
-        jnp.logical_and(core_names == core_id(m >> 3, m & 3), (n >> 6) == ((m >> 2) & 1))
-    )
-    n16 = iota((16, 512), 1)
-    ids16 = core_id(n16 >> 4, n16 & 3)
-    group = (n16 >> 2) & 3
-    for p, held in enumerate((names[0:16, :], names_in[3, 0:16, :])):
-        named = jnp.concatenate([held] * 4, axis=1) == ids16
-        for half in range(2):
-            for kind in range(2):
-                at = p * 64 + half * 32 + kind * 16
-                hot_down[at : at + 16, :] = one_hot(
-                    jnp.logical_and(named, group == kind * 2 + half)
-                )
+    def x_tables():
+        quarter = iota((1, 128), 1) >> 5
+        narrow = names[16:17, :]
+        for p in range(3):
+            narrow = jnp.where(quarter == p + 1, along_in[p], narrow)
+        narrow = jnp.concatenate([narrow, narrow], axis=1)
+        m = iota((128, 256), 0)
+        n = iota((128, 256), 1)
+        slot = m >> 3
+        ids = ((((slot >> 1) * 4 + x) * 2 + (slot & 1)) * 4) + (m & 3)
+        hot_up[...] = one_hot(jnp.logical_and(narrow == ids, (n >> 7) == ((m >> 2) & 1)))
+
+    def down_tables():
+        n16 = iota((16, 512), 1)
+        ids16 = core_id(n16 >> 4, n16 & 3)
+        group = (n16 >> 2) & 3
+        for p, held in enumerate((names[0:16, :], names_in[0:16, :])):
+            named = jnp.concatenate([held] * 4, axis=1) == ids16
+            for half in range(2):
+                for kind in range(2):
+                    at = p * 64 + half * 32 + kind * 16
+                    hot_down[at : at + 16, :] = one_hot(
+                        jnp.logical_and(named, group == kind * 2 + half)
+                    )
 
     def by_quarters(terms):
         return jnp.concatenate(
@@ -381,10 +398,22 @@
         wait_bytes(recv_a.at[t], recv_sem.at[DOWN_CORE + t])
         picked[...] = own + recv_a[t].astype(F32)
 
+    wait_bytes(names_in, recv_sem.at[NAMES_CORE])
+    core_tables()
+    pl.semaphore_wait(entered, 3)
+    to_owner_direct(0)
+    wait_bytes(along_in, recv_sem.at[NAMES])
+    x_tables()
     to_owner(0)
-    to_owner(1)
+    down_tables()
+
+    def turn(k, carry):
+        flipped[k] = tiles[k].T
+        return carry
+
+    lax.fori_loop(EARLY, TILES, turn, 0)
+    second_sum = own_total_direct(0)
     first_sum = own_total(0)
-    second_sum = own_total(1)
     row_first = 1.0 / jnp.sqrt(first_sum + EPSILON)
     row_factor = row_first / jnp.sqrt(row_first * second_sum + EPSILON)
     to_holders(0, row_first, row_factor)
@@ -408,20 +437,20 @@
         return jnp.concatenate([top, value - top], axis=0).astype(BF16)
 
     row_products(high_low(col_next), True)
-    stage_up(buf_a.at[2])
-    send_up(2)
+    stage_up(buf_a.at[1], row_parts)
+    send_up(1)
     unit = jnp.maximum(-primal_rate * cost_scaled, 0.0)
     row_products(high_low(col_next * (2.0 * unit)), False)
-    stage_up(buf_c.at[0])
-    send_core(0)
-
+    stage_up(buf_c.at[1], row_parts)
+    send_core(1)
+
+    to_owner_direct(1)
     wait_bytes(scal_x, recv_sem.at[SCAL_X])
     scal_out[...] = scal[...] + scal_x[0] + scal_x[1] + scal_x[2]
     for index, entry in enumerate(PLANE):
         pg, pz, py, pc = plane(entry)
         send(scal_out, scal_in.at[index], SCAL_PLANE, (pg, pz, py, x, pc))
-    to_owner_direct(0)
-    to_owner(2)
+    to_owner(1)
     wait_bytes(scal_in, recv_sem.at[SCAL_PLANE])
     both_squares = scal_out[...] + jnp.sum(scal_in[...], axis=0)
     wide_count = 64
@@ -431,8 +460,8 @@
     cost_hat = cost_scaled * cost_gain
     demand_hat = demand_scaled * demand_gain
 
-    dual_rate = dual_step[()] / (row_factor * own_total(2) + EPSILON)
-    dual = dual_rate * (demand_hat - row_factor * (own_total_direct(0) * cost_gain))
+    dual_rate = dual_step[()] / (row_factor * own_total(1) + EPSILON)
+    dual = dual_rate * (demand_hat - row_factor * (own_total_direct(1) * cost_gain))
     weighted = row_factor * dual.astype(BF16).astype(F32)
     top = weighted.astype(BF16).astype(F32)
     to_holders(1, top, weighted - top)
@@ -443,22 +472,24 @@
     primal_out[...] = primal_next
     bar = (2.0 * primal_next - primal).astype(BF16).astype(F32)
     row_products(high_low(col_next * bar), False)
-    stage_up(buf_c.at[1])
-    send_core(1)
-    to_owner_direct(1)
-    dual_next = dual + dual_rate * (demand_hat - row_factor * own_total_direct(1))
+    stage_up(buf_c.at[2], row_parts)
+    send_core(2)
+    to_owner_direct(2)
+    dual_next = dual + dual_rate * (demand_hat - row_factor * own_total_direct(2))
     dual_out[:, 0:128] = dual_next[0:4]
     dual_out[:, 128:256] = dual_next[4:8]
 
-    wait_bytes(names_in, send_sem.at[NAMES])
+    wait_bytes(along_in, send_sem.at[NAMES])
+    wait_bytes(names_in, send_sem.at[NAMES_CORE])
     wait_bytes(scal_x, send_sem.at[SCAL_X])
     wait_bytes(scal_in, send_sem.at[SCAL_PLANE])
-    for q in range(3):
+    for q in range(2):
         wait_bytes(buf_a.at[q, 1:4], send_sem.at[UP_X + q])
         wait_bytes(recv_b.at[q], send_sem.at[UP_PLANE + q])
-    for t in range(2):
+    for t in range(3):
         wait_bytes(buf_c.at[t, 1], send_sem.at[UP_CORE + t])
         wait_bytes(recv_c.at[t], send_sem.at[UP_ALL + t])
+    for t in range(2):
         wait_bytes(recv_c.at[t], send_sem.at[DOWN_ALL + t])
         wait_bytes(recv_a.at[t], send_sem.at[DOWN_CORE + t])
 
@@ -489,15 +520,18 @@
             pltpu.VMEM((TILES, 512, 256), BF16),
             pltpu.VMEM((TILES, 256, 512), BF16),
             pltpu.VMEM((24, 128), jnp.int32),
-            pltpu.VMEM((4, 24, 128), jnp.int32),
+            pltpu.VMEM((24, 128), jnp.int32),
+            pltpu.VMEM((1, 128), jnp.int32),
+            pltpu.VMEM((3, 1, 128), jnp.int32),
+            pltpu.VMEM((16, 512), F32),
             pltpu.VMEM((16, 512), F32),
             pltpu.VMEM((16, 256), F32),
-            pltpu.VMEM((3, 4, 32, 512), BF16),
-            pltpu.VMEM((3, 16, 8, 256), F32),
-            pltpu.VMEM((3, 31, 8, 128), F32),
-            pltpu.VMEM((2, 2, 32, 512), BF16),
-            pltpu.VMEM((2, 32, 8, 256), F32),
-            pltpu.VMEM((2, 63, 8, 128), F32),
+            pltpu.VMEM((2, 4, 32, 512), BF16),
+            pltpu.VMEM((2, 16, 8, 256), F32),
+            pltpu.VMEM((2, 31, 8, 128), F32),
+            pltpu.VMEM((3, 2, 32, 512), BF16),
+            pltpu.VMEM((3, 32, 8, 256), F32),
+            pltpu.VMEM((3, 63, 8, 128), F32),
             pltpu.VMEM((2, 16, 128), BF16),
             pltpu.VMEM((2, 2, 32, 16, 128), BF16),
             pltpu.VMEM((2, 2, 32, 512), BF16),
@@ -513,6 +547,7 @@
             pltpu.VMEM((8, 128), F32),
             pltpu.SemaphoreType.DMA((TILES // LOAD,)),
             pltpu.SemaphoreType.DMA((4,)),
+            pltpu.SemaphoreType.REGULAR,
             pltpu.SemaphoreType.DMA((STAGES,)),
             pltpu.SemaphoreType.DMA((STAGES,)),
         ],

time: 59.7 us -> 57.8 us (0.968)
  Pallas kernels: 57.6 us -> 55.8 us
    pallas_call x1, Pallas kernels: 57 us -> 55.2 us  [on_device(): pl.pallas_call(kernel, out_shape=tuple((pltpu.VMEM(shape.shape, F32) for...]
where the time goes in v4:
time: 57.8 us; the launch traced here: 57.7 us
  Pallas kernels  55.8 us (97%)
  between operations  1.93 us (3%)
    pallas_call x1, Pallas kernels, on_device(): pl.pallas_call(kernel, out_shape=tuple((pltpu.VMEM(shape.shape, F32) for...  55.2 us

profile of v4, /device:TPU:0, one launch (start us, length us, event | category | flops | bytes accessed | tf_op | source)
XLA Modules:
  0.0 57.7 jit_solution(15399163491512298107)
XLA Ops:
  1.9 55.2 %shard_map.86 = (f32[8,256]{1,0:T(8,128)S(1)}, f32[4,256]{1,0:T(4,128)S(1)}) custom-call(s32[16]{0:T(128)} %rows_hbm.1, s32[16]{0:T(128)} %cols_hbm.1, f32[]{:T(128)S(6)} %copy.9.primal_step, f32[]{:T(128)S(6)} %copy.10.dual_step, bf16[16,512,256]{2,1,0:T(8,128)(2,1)} %tiles_hbm.1, f32[8,256]{1,0:T(8,128)} %objective_hbm.1, f32[4,256]{1,0:T(4,128)} %demand_hbm.1), custom_call_target="tpu_custom_call" | custom-call | tf_op jit(solution)/shard_map/pallas_call | solution.py:510
  57.1 0.6 %shard_map.87 = (f32[8,256]{1,0:T(8,128)}, f32[4,256]{1,0:T(4,128)}) custom-call(f32[8,256]{1,0:T(8,128)S(1)} %get-tuple-element.4.primal, f32[4,256]{1,0:T(4,128)S(1)} %get-tuple-element.5.dual), custom_call_target="tpu_custom_call" | custom-call | tf_op jit(solution)/shard_map/pallas_call | solution.py:565

commit v5 on v4

--- a/solution.py
+++ b/solution.py
@@ -95,14 +95,21 @@
     buf_c,
     send_c,
     recv_c,
+    send_one,
+    recv_last,
     pay,
     rows,
     sel,
     recv_a,
+    pay_one,
+    rows_one,
+    sel_one,
+    recv_one,
     picked,
     hot_up,
     hot_core,
     hot_down,
+    hot_one,
     scal,
     scal_x,
     scal_out,
@@ -242,15 +249,16 @@
 
         lax.fori_loop(0, TILES // CHUNK, body, 0)
 
-    def column_products(magnitude):
+    def column_products(kinds, magnitude):
         def body(step, total):
             lefts = []
             for j in range(CHUNK):
                 k = step * CHUNK + j
                 mine = eight_wide == column_of(k)
                 pieces = [
-                    jnp.where(mine, picked[pl.ds(kind * 16 + k, 1), :], 0.0) for kind in range(2)
-                ]
+                    jnp.where(mine, picked[pl.ds(kind * 16 + k, 1), :], 0.0)
+                    for kind in range(kinds)
+                ] + [jnp.zeros((8, 512), F32)] * (2 - kinds)
                 lefts.append(jnp.concatenate(pieces, axis=0).astype(BF16))
             block = tiles[pl.ds(step * CHUNK, CHUNK)].reshape(CHUNK * 512, 256)
             if magnitude:
@@ -314,6 +322,15 @@
         hot_up[...] = one_hot(jnp.logical_and(narrow == ids, (n >> 7) == ((m >> 2) & 1)))
 
     def down_tables():
+        n8 = iota((16, 256), 1)
+        ids8 = core_id(n8 >> 3, n8 & 3)
+        for p, held in enumerate((names[0:16, :], names_in[0:16, :])):
+            named = jnp.concatenate([held] * 2, axis=1) == ids8
+            for half in range(2):
+                at = p * 32 + half * 16
+                hot_one[at : at + 16, :] = one_hot(
+                    jnp.logical_and(named, ((n8 >> 2) & 1) == half)
+                )
         n16 = iota((16, 512), 1)
         ids16 = core_id(n16 >> 4, n16 & 3)
         group = (n16 >> 2) & 3
@@ -356,52 +373,52 @@
         wait_bytes(recv_b.at[q], recv_sem.at[UP_PLANE + q])
         return mine + jnp.sum(recv_b[q], axis=0)
 
-    def to_owner_direct(t):
+    def to_owner_direct(t, out, into):
         wait_bytes(buf_c.at[t, 1], recv_sem.at[UP_CORE + t])
         terms = by_quarters(buf_c[t].reshape(64, 512))
-        send_c[t] = dot(hot_core[...], terms).reshape(32, 8, 256)
+        dense = dot(hot_core[...], terms)
+        for half in range(2):
+            part = dense[:, half * 128 : (half + 1) * 128].reshape(32, 8, 128)
+            out[half] = part.astype(out.dtype)
         for index, entry in enumerate(CHIPS):
             pg, pz, py, px = chip(entry)
             target = (pz * 4 + py) * 4 + px
-            lanes = pl.ds(pl.multiple_of(pg * 128, 128), 128)
-            send(
-                send_c.at[t, target, :, lanes],
-                recv_c.at[t, index],
-                UP_ALL + t,
-                (pg, pz, py, px, c),
-            )
-
-    def own_total_direct(t):
-        mine = send_c[t, chip_me]
-        mine = jnp.where(g == 0, mine[:, 0:128], mine[:, 128:256])
-        wait_bytes(recv_c.at[t], recv_sem.at[UP_ALL + t])
-        return mine + jnp.sum(recv_c[t], axis=0)
-
-    def to_holders(t, first, second):
-        pay[t] = jnp.concatenate([first, second], axis=0).astype(BF16)
+            send(out.at[pg, target], into.at[index], UP_ALL + t, (pg, pz, py, px, c))
+
+    def own_total_direct(t, out, into):
+        mine = out[g, chip_me].astype(F32)
+        wait_bytes(into, recv_sem.at[UP_ALL + t])
+        return mine + jnp.sum(into[...].astype(F32), axis=0)
+
+    def to_holders(t, values, pay, rows, hot, sel, recv):
+        pay[...] = values.astype(BF16)
         for entry in CHIPS:
             pg, pz, py, px = chip(entry)
-            send(pay.at[t], rows.at[t, g, chip_me], DOWN_ALL + t, (pg, pz, py, px, c))
-        pltpu.make_async_copy(
-            pay.at[t], rows.at[t, g, chip_me], recv_sem.at[DOWN_ALL + t]
-        ).start()
-        wait_bytes(rows.at[t], recv_sem.at[DOWN_ALL + t])
+            send(pay, rows.at[g, chip_me], DOWN_ALL + t, (pg, pz, py, px, c))
+        pltpu.make_async_copy(pay, rows.at[g, chip_me], recv_sem.at[DOWN_ALL + t]).start()
+        wait_bytes(rows, recv_sem.at[DOWN_ALL + t])
+        height = pay.shape[0] * 2
+        held = [
+            rows[half].astype(F32).reshape(32 * pay.shape[0], 128).astype(BF16)
+            for half in range(2)
+        ]
+
         for half in range(2):
-            chosen = dot(hot_down[...], rows[t, half].reshape(512, 128)).astype(BF16)
+            chosen = dot(hot[...], held[half]).astype(BF16)
             for p in range(2):
                 for quarter in range(2):
                     at = (half * 2 + quarter) * 128
-                    begin = p * 64 + quarter * 32
-                    sel[t, p, :, at : at + 128] = chosen[begin : begin + 32]
-        send(sel.at[t, 1], recv_a.at[t], DOWN_CORE + t, other_core)
-        own = sel[t, 0].astype(F32)
-        wait_bytes(recv_a.at[t], recv_sem.at[DOWN_CORE + t])
-        picked[...] = own + recv_a[t].astype(F32)
+                    begin = (p * 2 + quarter) * height
+                    sel[p, :, at : at + 128] = chosen[begin : begin + height]
+        send(sel.at[1], recv, DOWN_CORE + t, other_core)
+        own = sel[0].astype(F32)
+        wait_bytes(recv, recv_sem.at[DOWN_CORE + t])
+        picked[0:height, :] = own + recv[...].astype(F32)
 
     wait_bytes(names_in, recv_sem.at[NAMES_CORE])
     core_tables()
     pl.semaphore_wait(entered, 3)
-    to_owner_direct(0)
+    to_owner_direct(0, send_c.at[0], recv_c.at[0])
     wait_bytes(along_in, recv_sem.at[NAMES])
     x_tables()
     to_owner(0)
@@ -412,13 +429,14 @@
         return carry
 
     lax.fori_loop(EARLY, TILES, turn, 0)
-    second_sum = own_total_direct(0)
+    second_sum = own_total_direct(0, send_c.at[0], recv_c.at[0])
     first_sum = own_total(0)
     row_first = 1.0 / jnp.sqrt(first_sum + EPSILON)
     row_factor = row_first / jnp.sqrt(row_first * second_sum + EPSILON)
-    to_holders(0, row_first, row_factor)
-
-    sums = column_products(True)
+    values = jnp.concatenate([row_first, row_factor], axis=0)
+    to_holders(0, values, pay, rows, hot_down, sel, recv_a)
+
+    sums = column_products(2, True)
     col_next = col_factor / jnp.sqrt(col_factor * sums[0:8] + EPSILON)
     col_abs = col_next * sums[8:16]
     primal_rate = primal_step[()] / (col_abs + EPSILON)
@@ -444,7 +462,7 @@
     stage_up(buf_c.at[1], row_parts)
     send_core(1)
 
-    to_owner_direct(1)
+    to_owner_direct(1, send_c.at[1], recv_c.at[1])
     wait_bytes(scal_x, recv_sem.at[SCAL_X])
     scal_out[...] = scal[...] + scal_x[0] + scal_x[1] + scal_x[2]
     for index, entry in enumerate(PLANE):
@@ -461,21 +479,22 @@
     demand_hat = demand_scaled * demand_gain
 
     dual_rate = dual_step[()] / (row_factor * own_total(1) + EPSILON)
-    dual = dual_rate * (demand_hat - row_factor * (own_total_direct(1) * cost_gain))
+    pushed = row_factor * (own_total_direct(1, send_c.at[1], recv_c.at[1]) * cost_gain)
+    dual = dual_rate * (demand_hat - pushed)
     weighted = row_factor * dual.astype(BF16).astype(F32)
-    top = weighted.astype(BF16).astype(F32)
-    to_holders(1, top, weighted - top)
-
-    sums = column_products(False)
-    pulled = col_next * (sums[0:8] + sums[8:16])
+    to_holders(1, weighted, pay_one, rows_one, hot_one, sel_one, recv_one)
+
+    sums = column_products(1, False)
+    pulled = col_next * sums[0:8]
     primal_next = jnp.maximum(primal - primal_rate * (cost_hat - pulled), 0.0)
     primal_out[...] = primal_next
     bar = (2.0 * primal_next - primal).astype(BF16).astype(F32)
-    row_products(high_low(col_next * bar), False)
+    row_products(high_low(col_next * (bar - 3.0 * primal)), False)
     stage_up(buf_c.at[2], row_parts)
     send_core(2)
-    to_owner_direct(2)
-    dual_next = dual + dual_rate * (demand_hat - row_factor * own_total_direct(2))
+    to_owner_direct(2, send_one, recv_last)
+    rest = row_factor * own_total_direct(2, send_one, recv_last)
+    dual_next = dual + dual_rate * (demand_hat - (1.5 * pushed + rest))
     dual_out[:, 0:128] = dual_next[0:4]
     dual_out[:, 128:256] = dual_next[4:8]
 
@@ -486,12 +505,12 @@
     for q in range(2):
         wait_bytes(buf_a.at[q, 1:4], send_sem.at[UP_X + q])
         wait_bytes(recv_b.at[q], send_sem.at[UP_PLANE + q])
-    for t in range(3):
+    for t, into in enumerate((recv_c.at[0], recv_c.at[1], recv_last)):
         wait_bytes(buf_c.at[t, 1], send_sem.at[UP_CORE + t])
-        wait_bytes(recv_c.at[t], send_sem.at[UP_ALL + t])
-    for t in range(2):
-        wait_bytes(recv_c.at[t], send_sem.at[DOWN_ALL + t])
-        wait_bytes(recv_a.at[t], send_sem.at[DOWN_CORE + t])
+        wait_bytes(into, send_sem.at[UP_ALL + t])
+    for t, (into, recv) in enumerate(((recv_c.at[0], recv_a), (recv_last, recv_one))):
+        wait_bytes(into, send_sem.at[DOWN_ALL + t])
+        wait_bytes(recv, send_sem.at[DOWN_CORE + t])
 
 
 def hand_over(primal, dual, primal_out, dual_out):
@@ -530,16 +549,23 @@
             pltpu.VMEM((2, 16, 8, 256), F32),
             pltpu.VMEM((2, 31, 8, 128), F32),
             pltpu.VMEM((3, 2, 32, 512), BF16),
-            pltpu.VMEM((3, 32, 8, 256), F32),
-            pltpu.VMEM((3, 63, 8, 128), F32),
-            pltpu.VMEM((2, 16, 128), BF16),
-            pltpu.VMEM((2, 2, 32, 16, 128), BF16),
-            pltpu.VMEM((2, 2, 32, 512), BF16),
+            pltpu.VMEM((2, 2, 32, 8, 128), F32),
+            pltpu.VMEM((2, 63, 8, 128), F32),
+            pltpu.VMEM((2, 32, 8, 128), BF16),
+            pltpu.VMEM((63, 8, 128), BF16),
+            pltpu.VMEM((16, 128), BF16),
+            pltpu.VMEM((2, 32, 16, 128), BF16),
             pltpu.VMEM((2, 32, 512), BF16),
+            pltpu.VMEM((32, 512), BF16),
+            pltpu.VMEM((8, 128), BF16),
+            pltpu.VMEM((2, 32, 8, 128), BF16),
+            pltpu.VMEM((2, 16, 512), BF16),
+            pltpu.VMEM((16, 512), BF16),
             pltpu.VMEM((32, 512), F32),
             pltpu.VMEM((128, 256), BF16),
             pltpu.VMEM((256, 128), BF16),
             pltpu.VMEM((128, 512), BF16),
+            pltpu.VMEM((64, 256), BF16),
             pltpu.VMEM((1, 128), F32),
             pltpu.VMEM((3, 1, 128), F32),
             pltpu.VMEM((1, 128), F32),

time: 57.8 us -> 56.7 us (0.981)
  Pallas kernels: 55.8 us -> 54.6 us
    pallas_call x1, Pallas kernels: 55.2 us -> 54 us  [on_device(): pl.pallas_call(kernel, out_shape=tuple((pltpu.VMEM(shape.shape, F32) for...]
where the time goes in v5:
time: 56.7 us; the launch traced here: 56.5 us
  Pallas kernels  54.6 us (96%)
  between operations  1.93 us (3%)
    pallas_call x1, Pallas kernels, on_device(): pl.pallas_call(kernel, out_shape=tuple((pltpu.VMEM(shape.shape, F32) for...  54 us

profile of v5, /device:TPU:0, one launch (start us, length us, event | category | flops | bytes accessed | tf_op | source)
XLA Modules:
  0.0 56.5 jit_solution(4816807193343124179)
XLA Ops:
  1.9 54.0 %shard_map.86 = (f32[8,256]{1,0:T(8,128)S(1)}, f32[4,256]{1,0:T(4,128)S(1)}) custom-call(s32[16]{0:T(128)} %rows_hbm.1, s32[16]{0:T(128)} %cols_hbm.1, f32[]{:T(128)S(6)} %copy.9.primal_step, f32[]{:T(128)S(6)} %copy.10.dual_step, bf16[16,512,256]{2,1,0:T(8,128)(2,1)} %tiles_hbm.1, f32[8,256]{1,0:T(8,128)} %objective_hbm.1, f32[4,256]{1,0:T(4,128)} %demand_hbm.1), custom_call_target="tpu_custom_call" | custom-call | tf_op jit(solution)/shard_map/pallas_call | solution.py:529
  55.9 0.6 %shard_map.87 = (f32[8,256]{1,0:T(8,128)}, f32[4,256]{1,0:T(4,128)}) custom-call(f32[8,256]{1,0:T(8,128)S(1)} %get-tuple-element.4.primal, f32[4,256]{1,0:T(4,128)S(1)} %get-tuple-element.5.dual), custom_call_target="tpu_custom_call" | custom-call | tf_op jit(solution)/shard_map/pallas_call | solution.py:591

commit v6 on v5

--- a/solution.py
+++ b/solution.py
@@ -15,7 +15,7 @@
 F32 = jnp.float32
 BF16 = jnp.bfloat16
 TILES = 16
-CHUNK = 4
+CHUNK = 8
 LOAD = 2
 EARLY = 8
 
@@ -284,12 +284,12 @@
         return carry
 
     lax.fori_loop(0, EARLY // CHUNK, functools.partial(both_sums, True), 0)
+    pl.semaphore_wait(barrier, 34)
+    for step in (2, 1, 3):
+        pl.semaphore_signal(entered, inc=1, device_id=x_device(step), device_id_type=MESH)
     lax.fori_loop(EARLY // CHUNK, TILES // CHUNK, functools.partial(both_sums, False), 0)
     stage_up(buf_c.at[0], row_parts)
     stage_up(buf_a.at[0], first_parts)
-    pl.semaphore_wait(barrier, 34)
-    for step in (2, 1, 3):
-        pl.semaphore_signal(entered, inc=1, device_id=x_device(step), device_id_type=MESH)
     send(names, names_in, NAMES_CORE, other_core)
     send_core(0)
     send_up(0)
@@ -462,12 +462,12 @@
     stage_up(buf_c.at[1], row_parts)
     send_core(1)
 
-    to_owner_direct(1, send_c.at[1], recv_c.at[1])
     wait_bytes(scal_x, recv_sem.at[SCAL_X])
     scal_out[...] = scal[...] + scal_x[0] + scal_x[1] + scal_x[2]
     for index, entry in enumerate(PLANE):
         pg, pz, py, pc = plane(entry)
         send(scal_out, scal_in.at[index], SCAL_PLANE, (pg, pz, py, x, pc))
+    to_owner_direct(1, send_c.at[1], recv_c.at[1])
     to_owner(1)
     wait_bytes(scal_in, recv_sem.at[SCAL_PLANE])
     both_squares = scal_out[...] + jnp.sum(scal_in[...], axis=0)

time: 56.7 us -> 55.6 us (0.981)
  Pallas kernels: 54.6 us -> 53.5 us
    pallas_call x1, Pallas kernels: 54 us -> 52.9 us  [on_device(): pl.pallas_call(kernel, out_shape=tuple((pltpu.VMEM(shape.shape, F32) for...]
where the time goes in v6:
time: 55.6 us; the launch traced here: 55.5 us
  Pallas kernels  53.5 us (96%)
  between operations  1.93 us (3%)
    pallas_call x1, Pallas kernels, on_device(): pl.pallas_call(kernel, out_shape=tuple((pltpu.VMEM(shape.shape, F32) for...  52.9 us

profile of v6, /device:TPU:0, one launch (start us, length us, event | category | flops | bytes accessed | tf_op | source)
XLA Modules:
  0.0 55.5 jit_solution(4342007432416282932)
XLA Ops:
  1.9 52.9 %shard_map.86 = (f32[8,256]{1,0:T(8,128)S(1)}, f32[4,256]{1,0:T(4,128)S(1)}) custom-call(s32[16]{0:T(128)} %rows_hbm.1, s32[16]{0:T(128)} %cols_hbm.1, f32[]{:T(128)S(6)} %copy.9.primal_step, f32[]{:T(128)S(6)} %copy.10.dual_step, bf16[16,512,256]{2,1,0:T(8,128)(2,1)} %tiles_hbm.1, f32[8,256]{1,0:T(8,128)} %objective_hbm.1, f32[4,256]{1,0:T(4,128)} %demand_hbm.1), custom_call_target="tpu_custom_call" | custom-call | tf_op jit(solution)/shard_map/pallas_call | solution.py:529
  54.9 0.6 %shard_map.87 = (f32[8,256]{1,0:T(8,128)}, f32[4,256]{1,0:T(4,128)}) custom-call(f32[8,256]{1,0:T(8,128)S(1)} %get-tuple-element.4.primal, f32[4,256]{1,0:T(4,128)S(1)} %get-tuple-element.5.dual), custom_call_target="tpu_custom_call" | custom-call | tf_op jit(solution)/shard_map/pallas_call | solution.py:591

commit v7 on v6

--- a/solution.py
+++ b/solution.py
@@ -20,9 +20,9 @@
 EARLY = 8
 
 NAMES, NAMES_CORE, SCAL_X, SCAL_PLANE = range(4)
-UP_X, UP_PLANE = 4, 6
-UP_CORE, UP_ALL, DOWN_ALL, DOWN_CORE = 8, 11, 14, 16
-STAGES = 18
+UP_X, UP_PLANE = 4, 5
+UP_CORE, UP_ALL, DOWN_ALL, DOWN_CORE = 6, 10, 14, 17
+STAGES = 20
 
 
 def offsets():
@@ -101,15 +101,10 @@
     rows,
     sel,
     recv_a,
-    pay_one,
-    rows_one,
-    sel_one,
-    recv_one,
     picked,
     hot_up,
     hot_core,
     hot_down,
-    hot_one,
     scal,
     scal_x,
     scal_out,
@@ -249,23 +244,20 @@
 
         lax.fori_loop(0, TILES // CHUNK, body, 0)
 
-    def column_products(kinds, magnitude):
+    def column_products(magnitude):
         def body(step, total):
             lefts = []
             for j in range(CHUNK):
                 k = step * CHUNK + j
-                mine = eight_wide == column_of(k)
-                pieces = [
-                    jnp.where(mine, picked[pl.ds(kind * 16 + k, 1), :], 0.0)
-                    for kind in range(kinds)
-                ] + [jnp.zeros((8, 512), F32)] * (2 - kinds)
+                mine = jnp.where(eight_wide == column_of(k), picked[pl.ds(k, 1), :], 0.0)
+                pieces = [mine, jnp.zeros((8, 512), F32)]
                 lefts.append(jnp.concatenate(pieces, axis=0).astype(BF16))
             block = tiles[pl.ds(step * CHUNK, CHUNK)].reshape(CHUNK * 512, 256)
             if magnitude:
                 block = jnp.abs(block)
             return total + dot(jnp.concatenate(lefts, axis=1), block)
 
-        return lax.fori_loop(0, TILES // CHUNK, body, jnp.zeros((16, 256), F32))
+        return lax.fori_loop(0, TILES // CHUNK, body, jnp.zeros((16, 256), F32))[0:8]
 
     col_factor = 1.0 / jnp.sqrt(col_total + EPSILON)
     left = jnp.concatenate([col_factor, jnp.where(eight == 0, 1.0, 0.0)], axis=0).astype(BF16)
@@ -288,8 +280,8 @@
     for step in (2, 1, 3):
         pl.semaphore_signal(entered, inc=1, device_id=x_device(step), device_id_type=MESH)
     lax.fori_loop(EARLY // CHUNK, TILES // CHUNK, functools.partial(both_sums, False), 0)
-    stage_up(buf_c.at[0], row_parts)
-    stage_up(buf_a.at[0], first_parts)
+    stage_up(buf_c.at[0], first_parts)
+    stage_up(buf_a.at[0], row_parts)
     send(names, names_in, NAMES_CORE, other_core)
     send_core(0)
     send_up(0)
@@ -328,20 +320,9 @@
             named = jnp.concatenate([held] * 2, axis=1) == ids8
             for half in range(2):
                 at = p * 32 + half * 16
-                hot_one[at : at + 16, :] = one_hot(
+                hot_down[at : at + 16, :] = one_hot(
                     jnp.logical_and(named, ((n8 >> 2) & 1) == half)
                 )
-        n16 = iota((16, 512), 1)
-        ids16 = core_id(n16 >> 4, n16 & 3)
-        group = (n16 >> 2) & 3
-        for p, held in enumerate((names[0:16, :], names_in[0:16, :])):
-            named = jnp.concatenate([held] * 4, axis=1) == ids16
-            for half in range(2):
-                for kind in range(2):
-                    at = p * 64 + half * 32 + kind * 16
-                    hot_down[at : at + 16, :] = one_hot(
-                        jnp.logical_and(named, group == kind * 2 + half)
-                    )
 
     def by_quarters(terms):
         return jnp.concatenate(
@@ -390,30 +371,31 @@
         wait_bytes(into, recv_sem.at[UP_ALL + t])
         return mine + jnp.sum(into[...].astype(F32), axis=0)
 
-    def to_holders(t, values, pay, rows, hot, sel, recv):
-        pay[...] = values.astype(BF16)
+    def gather(t, values):
+        pay[t] = values.astype(BF16)
         for entry in CHIPS:
             pg, pz, py, px = chip(entry)
-            send(pay, rows.at[g, chip_me], DOWN_ALL + t, (pg, pz, py, px, c))
-        pltpu.make_async_copy(pay, rows.at[g, chip_me], recv_sem.at[DOWN_ALL + t]).start()
-        wait_bytes(rows, recv_sem.at[DOWN_ALL + t])
-        height = pay.shape[0] * 2
-        held = [
-            rows[half].astype(F32).reshape(32 * pay.shape[0], 128).astype(BF16)
-            for half in range(2)
-        ]
-
+            send(pay.at[t], rows.at[t, g, chip_me], DOWN_ALL + t, (pg, pz, py, px, c))
+        pltpu.make_async_copy(
+            pay.at[t], rows.at[t, g, chip_me], recv_sem.at[DOWN_ALL + t]
+        ).start()
+
+    def pick(t):
+        wait_bytes(rows.at[t], recv_sem.at[DOWN_ALL + t])
         for half in range(2):
-            chosen = dot(hot[...], held[half]).astype(BF16)
+            held = rows[t, half].astype(F32).reshape(256, 128).astype(BF16)
+            chosen = dot(hot_down[...], held).astype(BF16)
             for p in range(2):
                 for quarter in range(2):
                     at = (half * 2 + quarter) * 128
-                    begin = (p * 2 + quarter) * height
-                    sel[p, :, at : at + 128] = chosen[begin : begin + height]
-        send(sel.at[1], recv, DOWN_CORE + t, other_core)
-        own = sel[0].astype(F32)
-        wait_bytes(recv, recv_sem.at[DOWN_CORE + t])
-        picked[0:height, :] = own + recv[...].astype(F32)
+                    begin = (p * 2 + quarter) * 16
+                    sel[t, p, :, at : at + 128] = chosen[begin : begin + 16]
+        send(sel.at[t, 1], recv_a.at[t], DOWN_CORE + t, other_core)
+
+    def picked_rows(t):
+        own = sel[t, 0].astype(F32)
+        wait_bytes(recv_a.at[t], recv_sem.at[DOWN_CORE + t])
+        picked[...] = own + recv_a[t].astype(F32)
 
     wait_bytes(names_in, recv_sem.at[NAMES_CORE])
     core_tables()
@@ -429,17 +411,15 @@
         return carry
 
     lax.fori_loop(EARLY, TILES, turn, 0)
-    second_sum = own_total_direct(0, send_c.at[0], recv_c.at[0])
-    first_sum = own_total(0)
-    row_first = 1.0 / jnp.sqrt(first_sum + EPSILON)
-    row_factor = row_first / jnp.sqrt(row_first * second_sum + EPSILON)
-    values = jnp.concatenate([row_first, row_factor], axis=0)
-    to_holders(0, values, pay, rows, hot_down, sel, recv_a)
-
-    sums = column_products(2, True)
-    col_next = col_factor / jnp.sqrt(col_factor * sums[0:8] + EPSILON)
-    col_abs = col_next * sums[8:16]
-    primal_rate = primal_step[()] / (col_abs + EPSILON)
+    row_first = 1.0 / jnp.sqrt(own_total_direct(0, send_c.at[0], recv_c.at[0]) + EPSILON)
+    gather(0, row_first)
+    row_factor = row_first / jnp.sqrt(row_first * own_total(0) + EPSILON)
+    gather(1, row_factor)
+
+    pick(0)
+    picked_rows(0)
+    sums = column_products(True)
+    col_next = col_factor / jnp.sqrt(col_factor * sums + EPSILON)
     cost_scaled = col_next * objective[...]
     demand_scaled = row_factor * demand8[...]
 
@@ -454,21 +434,25 @@
         top = value.astype(BF16).astype(F32)
         return jnp.concatenate([top, value - top], axis=0).astype(BF16)
 
+    pick(1)
     row_products(high_low(col_next), True)
-    stage_up(buf_a.at[1], row_parts)
-    send_up(1)
-    unit = jnp.maximum(-primal_rate * cost_scaled, 0.0)
-    row_products(high_low(col_next * (2.0 * unit)), False)
     stage_up(buf_c.at[1], row_parts)
     send_core(1)
-
+    picked_rows(1)
+    col_abs = col_next * column_products(True)
+    primal_rate = primal_step[()] / (col_abs + EPSILON)
+    to_owner_direct(1, send_c.at[1], recv_c.at[1])
     wait_bytes(scal_x, recv_sem.at[SCAL_X])
     scal_out[...] = scal[...] + scal_x[0] + scal_x[1] + scal_x[2]
     for index, entry in enumerate(PLANE):
         pg, pz, py, pc = plane(entry)
         send(scal_out, scal_in.at[index], SCAL_PLANE, (pg, pz, py, x, pc))
-    to_owner_direct(1, send_c.at[1], recv_c.at[1])
-    to_owner(1)
+    unit = jnp.maximum(-primal_rate * cost_scaled, 0.0)
+    row_products(high_low(col_next * (2.0 * unit)), False)
+    stage_up(buf_c.at[2], row_parts)
+    send_core(2)
+
+    to_owner_direct(2, send_c.at[2], recv_c.at[2])
     wait_bytes(scal_in, recv_sem.at[SCAL_PLANE])
     both_squares = scal_out[...] + jnp.sum(scal_in[...], axis=0)
     wide_count = 64
@@ -478,22 +462,23 @@
     cost_hat = cost_scaled * cost_gain
     demand_hat = demand_scaled * demand_gain
 
-    dual_rate = dual_step[()] / (row_factor * own_total(1) + EPSILON)
-    pushed = row_factor * (own_total_direct(1, send_c.at[1], recv_c.at[1]) * cost_gain)
+    dual_rate = dual_step[()] / (row_factor * own_total_direct(1, send_c.at[1], recv_c.at[1]) + EPSILON)
+    pushed = row_factor * (own_total_direct(2, send_c.at[2], recv_c.at[2]) * cost_gain)
     dual = dual_rate * (demand_hat - pushed)
     weighted = row_factor * dual.astype(BF16).astype(F32)
-    to_holders(1, weighted, pay_one, rows_one, hot_one, sel_one, recv_one)
-
-    sums = column_products(1, False)
-    pulled = col_next * sums[0:8]
+    gather(2, weighted)
+    pick(2)
+    picked_rows(2)
+
+    pulled = col_next * column_products(False)
     primal_next = jnp.maximum(primal - primal_rate * (cost_hat - pulled), 0.0)
     primal_out[...] = primal_next
     bar = (2.0 * primal_next - primal).astype(BF16).astype(F32)
     row_products(high_low(col_next * (bar - 3.0 * primal)), False)
-    stage_up(buf_c.at[2], row_parts)
-    send_core(2)
-    to_owner_direct(2, send_one, recv_last)
-    rest = row_factor * own_total_direct(2, send_one, recv_last)
+    stage_up(buf_c.at[3], row_parts)
+    send_core(3)
+    to_owner_direct(3, send_one, recv_last)
+    rest = row_factor * own_total_direct(3, send_one, recv_last)
     dual_next = dual + dual_rate * (demand_hat - (1.5 * pushed + rest))
     dual_out[:, 0:128] = dual_next[0:4]
     dual_out[:, 128:256] = dual_next[4:8]
@@ -502,15 +487,14 @@
     wait_bytes(names_in, send_sem.at[NAMES_CORE])
     wait_bytes(scal_x, send_sem.at[SCAL_X])
     wait_bytes(scal_in, send_sem.at[SCAL_PLANE])
-    for q in range(2):
-        wait_bytes(buf_a.at[q, 1:4], send_sem.at[UP_X + q])
-        wait_bytes(recv_b.at[q], send_sem.at[UP_PLANE + q])
-    for t, into in enumerate((recv_c.at[0], recv_c.at[1], recv_last)):
+    wait_bytes(buf_a.at[0, 1:4], send_sem.at[UP_X])
+    wait_bytes(recv_b.at[0], send_sem.at[UP_PLANE])
+    for t, into in enumerate((recv_c.at[0], recv_c.at[1], recv_c.at[2], recv_last)):
         wait_bytes(buf_c.at[t, 1], send_sem.at[UP_CORE + t])
         wait_bytes(into, send_sem.at[UP_ALL + t])
-    for t, (into, recv) in enumerate(((recv_c.at[0], recv_a), (recv_last, recv_one))):
-        wait_bytes(into, send_sem.at[DOWN_ALL + t])
-        wait_bytes(recv, send_sem.at[DOWN_CORE + t])
+    for t in range(3):
+        wait_bytes(recv_last, send_sem.at[DOWN_ALL + t])
+        wait_bytes(recv_a.at[t], send_sem.at[DOWN_CORE + t])
 
 
 def hand_over(primal, dual, primal_out, dual_out):
@@ -545,26 +529,21 @@
             pltpu.VMEM((16, 512), F32),
             pltpu.VMEM((16, 512), F32),
             pltpu.VMEM((16, 256), F32),
-            pltpu.VMEM((2, 4, 32, 512), BF16),
-            pltpu.VMEM((2, 16, 8, 256), F32),
-            pltpu.VMEM((2, 31, 8, 128), F32),
-            pltpu.VMEM((3, 2, 32, 512), BF16),
-            pltpu.VMEM((2, 2, 32, 8, 128), F32),
-            pltpu.VMEM((2, 63, 8, 128), F32),
+            pltpu.VMEM((1, 4, 32, 512), BF16),
+            pltpu.VMEM((1, 16, 8, 256), F32),
+            pltpu.VMEM((1, 31, 8, 128), F32),
+            pltpu.VMEM((4, 2, 32, 512), BF16),
+            pltpu.VMEM((3, 2, 32, 8, 128), F32),
+            pltpu.VMEM((3, 63, 8, 128), F32),
             pltpu.VMEM((2, 32, 8, 128), BF16),
             pltpu.VMEM((63, 8, 128), BF16),
-            pltpu.VMEM((16, 128), BF16),
-            pltpu.VMEM((2, 32, 16, 128), BF16),
-            pltpu.VMEM((2, 32, 512), BF16),
-            pltpu.VMEM((32, 512), BF16),
-            pltpu.VMEM((8, 128), BF16),
-            pltpu.VMEM((2, 32, 8, 128), BF16),
-            pltpu.VMEM((2, 16, 512), BF16),
-            pltpu.VMEM((16, 512), BF16),
-            pltpu.VMEM((32, 512), F32),
+            pltpu.VMEM((3, 8, 128), BF16),
+            pltpu.VMEM((3, 2, 32, 8, 128), BF16),
+            pltpu.VMEM((3, 2, 16, 512), BF16),
+            pltpu.VMEM((3, 16, 512), BF16),
+            pltpu.VMEM((16, 512), F32),
             pltpu.VMEM((128, 256), BF16),
             pltpu.VMEM((256, 128), BF16),
-            pltpu.VMEM((128, 512), BF16),
             pltpu.VMEM((64, 256), BF16),
             pltpu.VMEM((1, 128), F32),
             pltpu.VMEM((3, 1, 128), F32),

time: 55.6 us -> 54.4 us (0.978)
  Pallas kernels: 53.5 us -> 52.4 us
    pallas_call x1, Pallas kernels: 52.9 us -> 51.8 us  [on_device(): pl.pallas_call(kernel, out_shape=tuple((pltpu.VMEM(shape.shape, F32) for...]
where the time goes in v7:
time: 54.4 us; the launch traced here: 54.3 us
  Pallas kernels  52.4 us (96%)
  between operations  1.93 us (4%)
    pallas_call x1, Pallas kernels, on_device(): pl.pallas_call(kernel, out_shape=tuple((pltpu.VMEM(shape.shape, F32) for...  51.8 us

profile of v7, /device:TPU:0, one launch (start us, length us, event | category | flops | bytes accessed | tf_op | source)
XLA Modules:
  0.0 54.3 jit_solution(10514082814432440646)
XLA Ops:
  1.9 51.8 %shard_map.86 = (f32[8,256]{1,0:T(8,128)S(1)}, f32[4,256]{1,0:T(4,128)S(1)}) custom-call(s32[16]{0:T(128)} %rows_hbm.1, s32[16]{0:T(128)} %cols_hbm.1, f32[]{:T(128)S(6)} %copy.9.primal_step, f32[]{:T(128)S(6)} %copy.10.dual_step, bf16[16,512,256]{2,1,0:T(8,128)(2,1)} %tiles_hbm.1, f32[8,256]{1,0:T(8,128)} %objective_hbm.1, f32[4,256]{1,0:T(4,128)} %demand_hbm.1), custom_call_target="tpu_custom_call" | custom-call | tf_op jit(solution)/shard_map/pallas_call | solution.py:513
  53.7 0.6 %shard_map.87 = (f32[8,256]{1,0:T(8,128)}, f32[4,256]{1,0:T(4,128)}) custom-call(f32[8,256]{1,0:T(8,128)S(1)} %get-tuple-element.4.primal, f32[4,256]{1,0:T(4,128)S(1)} %get-tuple-element.5.dual), custom_call_target="tpu_custom_call" | custom-call | tf_op jit(solution)/shard_map/pallas_call | solution.py:570
